TPU v7x, 32 devices: a whole 2x2x4 slice. The times are simulated.
32 devices in a mesh: dp: 16 (over z, y, x), ctx: 2 (over core).
Axes of the slice: x: 2, y: 2, z: 4, core: 2. Of those that a mesh axis runs over, the one named last changes fastest.
Arguments:
- inputs: bfloat16 [16, 256, 4096], P('dp', 'ctx'), may hold values from -6 to 6
- cotangent: bfloat16 [16, 256, 4096], P('dp', 'ctx'), may hold values from -6 to 6
- segment_ids: int32 [16, 256], P('dp'), may hold values from 0 to 3, never falling along the last dimension, each value on 1 to 128 neighbouring positions
- taps: bfloat16 [4096, 128], replicated, may hold values from -0.5 to 0.5
- skip_gain: float32 [4096], replicated, may hold values from 0.5 to 2
Outputs:
- input_grad: bfloat16 [16, 256, 4096], P('dp', 'ctx')
- taps_grad: float32 [4096, 128], P('ctx')
- skip_grad: float32 [4096], P('ctx')
Inputs may be any that keep to these rules, and one draw needn't show every extreme that they name: `segment_ids`: document numbers of a sequence never fall; each document has 1 to 128 positions, one exactly 128.
All inputs are finite; a program needn't handle non-finite values.
Results may differ from a plain program's by a relative error of at most 0.001.
Values may be sent and summed in bfloat16 or wider, within the bound.
No kernel may reach another device: no remote copies, remote signals or barrier semaphores. Data moves between devices by JAX's collectives and lax.ppermute only.
A program may use at most 128 MiB of HBM per device.

v0:
```python
import jax
import jax.numpy as jnp
from jax import lax
from jax.sharding import PartitionSpec as P


def padded(block, sides, width):
    for axis, dim in sides:
        count = lax.axis_size(axis)
        forward = [(i, i + 1) for i in range(count - 1)]
        backward = [(target, source) for source, target in forward]
        low = lax.ppermute(
            lax.slice_in_dim(block, block.shape[dim] - width, None, axis=dim), axis, forward
        )
        high = lax.ppermute(lax.slice_in_dim(block, 0, width, axis=dim), axis, backward)
        block = jnp.concatenate([low, block, high], axis=dim)
    return block


def shards(inputs, cotangent, segment_ids, taps, skip_gain):
    rows = inputs.shape[1]
    width = inputs.shape[2]
    kernel = taps.shape[1]
    reach = kernel - 1
    local_in = inputs[0]
    local_grad = cotangent[0]
    paired = jnp.stack([local_in, local_grad])
    extended = padded(paired, (("ctx", 1),), reach)
    below = extended[0, :reach]
    above = extended[1, rows + reach :]
    u_ext = jnp.concatenate([below, local_in], axis=0)
    g_ext = jnp.concatenate([local_grad, above], axis=0)
    anchor = lax.axis_index("ctx") * rows
    ids = segment_ids[0]
    ids_pad = jnp.concatenate(
        [jnp.full((reach,), -1, jnp.int32), ids, jnp.full((reach,), -1, jnp.int32)]
    )
    ids_here = lax.dynamic_slice_in_dim(ids_pad, anchor + reach, rows, 0)
    ids_lower = lax.dynamic_slice_in_dim(ids_pad, anchor, rows + reach, 0)
    ids_upper = lax.dynamic_slice_in_dim(ids_pad, anchor + reach, rows + reach, 0)
    block = min(kernel, 8)
    blocks = kernel // block
    taps32 = taps.astype(jnp.float32)
    g32 = local_grad.astype(jnp.float32)

    def one_block(accum, number):
        base = number * block
        lower_starts = [reach - base - offset for offset in range(block)]
        upper_starts = [base + offset for offset in range(block)]
        keep_before = (
            jnp.stack(
                [lax.dynamic_slice_in_dim(ids_lower, begin, rows, 0) for begin in lower_starts],
                axis=1,
            )
            == ids_here[:, None]
        )
        keep_after = (
            jnp.stack(
                [lax.dynamic_slice_in_dim(ids_upper, begin, rows, 0) for begin in upper_starts],
                axis=1,
            )
            == ids_here[:, None]
        )
        u_window = jnp.stack(
            [lax.dynamic_slice_in_dim(u_ext, begin, rows, 0) for begin in lower_starts], axis=1
        ).astype(jnp.float32)
        g_window = jnp.stack(
            [lax.dynamic_slice_in_dim(g_ext, begin, rows, 0) for begin in upper_starts], axis=1
        ).astype(jnp.float32)
        tap_cols = lax.dynamic_slice_in_dim(taps32, base, block, 1).T
        weighted = jnp.where(keep_after[:, :, None], g_window, 0.0) * tap_cols[None, :, :]
        accum = accum + jnp.sum(weighted, axis=1)
        masked = jnp.where(keep_before[:, :, None], u_window, 0.0) * g32[:, None, :]
        return (accum, jnp.sum(masked, axis=0))

    start = skip_gain[None, :] * g32
    accum, columns = lax.scan(one_block, start, jnp.arange(blocks, dtype=jnp.int32))
    input_grad = accum.astype(jnp.bfloat16)[None]
    taps_part = columns.reshape(kernel, width).T
    skip_part = jnp.einsum("tc,tc->c", local_grad, local_in, preferred_element_type=jnp.float32)
    summed = lax.psum((taps_part, skip_part), "dp")
    taps_share, skip_share = (
        lax.psum_scatter(summed[0], "ctx", scatter_dimension=0, tiled=True),
        lax.psum_scatter(summed[1], "ctx", scatter_dimension=0, tiled=True),
    )
    count = inputs.shape[0] * lax.axis_size("dp")
    return (input_grad, taps_share / count, skip_share / count)


def solution(mesh):
    return jax.shard_map(
        shards,
        mesh=mesh,
        in_specs=(P("dp", "ctx", None), P("dp", "ctx", None), P("dp", None), P(), P()),
        out_specs=(P("dp", "ctx", None), P("ctx", None), P("ctx")),
        check_vma=False,
    )
```

profile of v0, /device:TPU:0, one launch (start us, length us, event | category | flops | bytes accessed | tf_op | source)
XLA Modules:
  0.0 1068.1 jit_solution(8273173063244495362)
XLA Ops:
  7.2 3.6 copy.16
  10.8 3.6 copy.17
  14.4 10.6 pad_maximum_fusion.2
  26.4 5.7 collective-permute-start.1
  37.5 4.0 slice.18
  42.7 2.8 copy.33
  48.7 851.3 %while.16 = (s32[]{:T(128)}, f32[128,4096]{1,0:T(8,128)}, f32[16,8,4096]{2,1,0:T(8,128)}, s32[16]{0:T(128)S(1)}, s32[255]{0:T(256)S(1)}, /*index=5*/s32[128]{0:T...) while((s32[]{:T(128)}, f32[128,4096]{1,0:T(8,128)}, ...), condition=%wide.region_3.4_spmd, body=%wide.region_0.3_spmd.sunk | while | flops 33523780 | bytes 128694696 | solution.py:77
  84.1 3.1 bitcast_dynamic-update-slice_fusion.47
  88.4 7.3 multiply_reduce_fusion.4
  97.5 3.7 multiply_reduce_fusion.5
  137.3 3.1 bitcast_dynamic-update-slice_fusion.47
  141.6 7.3 multiply_reduce_fusion.4
  150.7 3.7 multiply_reduce_fusion.5
  190.5 3.1 bitcast_dynamic-update-slice_fusion.47
  194.8 7.3 multiply_reduce_fusion.4
  203.9 3.7 multiply_reduce_fusion.5
  243.7 3.1 bitcast_dynamic-update-slice_fusion.47
  248.0 7.3 multiply_reduce_fusion.4
  257.1 3.7 multiply_reduce_fusion.5
  270.2 2.7 bitcast_dynamic-update-slice_fusion.43
  296.9 3.1 bitcast_dynamic-update-slice_fusion.47
  301.2 7.3 multiply_reduce_fusion.4
  310.3 3.7 multiply_reduce_fusion.5
  323.4 2.7 bitcast_dynamic-update-slice_fusion.43
  350.1 3.1 bitcast_dynamic-update-slice_fusion.47
  354.4 7.3 multiply_reduce_fusion.4
  363.5 3.7 multiply_reduce_fusion.5
  376.6 2.7 bitcast_dynamic-update-slice_fusion.43
  403.3 3.1 bitcast_dynamic-update-slice_fusion.47
  407.6 7.3 multiply_reduce_fusion.4
  416.7 3.7 multiply_reduce_fusion.5
  429.8 2.7 bitcast_dynamic-update-slice_fusion.43
  456.5 3.1 bitcast_dynamic-update-slice_fusion.47
  460.8 7.3 multiply_reduce_fusion.4
  469.9 3.7 multiply_reduce_fusion.5
  483.1 2.7 bitcast_dynamic-update-slice_fusion.43
  509.7 3.1 bitcast_dynamic-update-slice_fusion.47
  514.0 7.3 multiply_reduce_fusion.4
  523.1 3.7 multiply_reduce_fusion.5
  536.3 2.7 bitcast_dynamic-update-slice_fusion.43
  562.9 3.1 bitcast_dynamic-update-slice_fusion.47
  567.3 7.3 multiply_reduce_fusion.4
  576.3 3.7 multiply_reduce_fusion.5
  616.1 3.1 bitcast_dynamic-update-slice_fusion.47
  620.5 7.3 multiply_reduce_fusion.4
  629.5 3.7 multiply_reduce_fusion.5
  669.3 3.1 bitcast_dynamic-update-slice_fusion.47
  673.7 7.3 multiply_reduce_fusion.4
  682.7 3.7 multiply_reduce_fusion.5
  722.5 3.1 bitcast_dynamic-update-slice_fusion.47
  726.9 7.3 multiply_reduce_fusion.4
  735.9 3.7 multiply_reduce_fusion.5
  775.7 3.1 bitcast_dynamic-update-slice_fusion.47
  780.1 7.3 multiply_reduce_fusion.4
  789.1 3.7 multiply_reduce_fusion.5
  828.9 3.1 bitcast_dynamic-update-slice_fusion.47
  833.3 7.3 multiply_reduce_fusion.4
  842.3 3.7 multiply_reduce_fusion.5
  882.1 3.1 bitcast_dynamic-update-slice_fusion.47
  886.5 7.3 multiply_reduce_fusion.4
  895.5 3.7 multiply_reduce_fusion.5
  902.8 3.4 all-reduce
  906.2 44.0 %psum.17 = f32[2048]{0:T(1024)S(1)} all-reduce(f32[2048]{0:T(1024)S(1)} %dynamic-slice.1), channel_id=1, replica_groups=mesh['dp'=16,'ctx'=2] {'dp'}, use_global_device_ids=true, to_apply=%region_6.7 | all-reduce | flops 2048 | bytes 16384 | tf_op jit(solution)/shard_map/psum | solution.py:81
  952.0 106.7 %all-reduce.3.cloned.1.call-done = f32[2048,128]{0,1:T(8,128)} async-done(((f32[2048,128]{0,1:T(8,128)}), f32[2048,128]{0,1:T(8,128)}) %all-reduce.3.cloned.1.call-update) | async-done | bytes 1048592 | tf_op jit(solution)/shard_map/psum | solution.py:81
  (628 shorter events, 615.4 us)
Async XLA Ops:
  7.2 943.0 %reduce-scatter.2.cloned.1.call-start = ((), (), s32[]{:S(2)}) async-start(), calls=%async_computation.1 | async-start | bytes 3145728 | tf_op jit(solution)/shard_map/reduce_scatter | solution.py:83
  14.4 17.7 %copy-start.10 = (s32[1,256]{1,0:T(1,128)S(1)}, s32[1,256]{1,0:T(1,128)}, u32[]{:S(2)}) copy-start(s32[1,256]{1,0:T(1,128)} %param.9) | copy-start | bytes 3076
  14.4 17.7 %copy-start.8 = (bf16[4096,128]{1,0:T(8,128)(2,1)S(1)}, bf16[4096,128]{1,0:T(8,128)(2,1)}, u32[]{:S(2)}) copy-start(bf16[4096,128]{1,0:T(8,128)(2,1)} %param.10) | copy-start | bytes 3145732
  25.0 9.4 copy-start.6
  25.0 12.5 %collective-permute-start = (bf16[2,127,4096]{2,0,1:T(2,128)(2,1)}, bf16[2,127,4096]{2,0,1:T(2,128)(2,1)}, u32[]{:S(2)}, u32[]{:S(2)}) collective-permute-start(bf16[2,127,4096]{2,0,1:T(2,128)(2,1)} %get-tuple-element.303), channel_id=1, source_target_pairs={{1,0},{3,2},{5,4},{7,6},{9,8},{11,10},{13,12},{15,14},{17,16},{19,... | collective-permute-start | bytes 6242312 | tf_op jit(solution)/shard_map/ppermute | solution.py:15
  26.4 16.2 %collective-permute-start.1 = (bf16[2,127,4096]{2,0,1:T(2,128)(2,1)}, bf16[2,127,4096]{2,0,1:T(2,128)(2,1)}, u32[]{:S(2)}, u32[]{:S(2)}) collective-permute-start(bf16[2,127,4096]{2,0,1:T(2,128)(2,1)} %get-tuple-element.302), channel_id=1, source_target_pairs={{0,1},{2,3},{4,5},{6,7},{8,9},{10,11},{12,13},{14,15},{16,17},{18,... | collective-permute-start | bytes 6242312 | tf_op jit(solution)/shard_map/ppermute | solution.py:12
  48.7 851.4 %copy-start.11 = (u32[32]{0:T(128)S(1)}, u32[32]{0:T(128)}, u32[]{:S(2)}) copy-start(u32[32]{0:T(128)} %constant.205) | copy-start | bytes 388
  57.4 10.2 copy-start.1
  73.9 10.2 copy-start
  87.3 9.0 slice-start
  88.4 7.9 slice-start.1
  110.6 10.2 copy-start.1
  127.1 10.2 copy-start
  140.5 9.0 slice-start
  141.6 7.9 slice-start.1
  163.8 10.2 copy-start.1
  180.3 10.2 copy-start
  193.7 9.0 slice-start
  194.8 7.9 slice-start.1
  217.0 10.2 copy-start.1
  233.5 10.2 copy-start
  246.9 9.0 slice-start
  248.0 7.9 slice-start.1
  270.2 10.2 copy-start.1
  286.7 10.2 copy-start
  300.1 9.0 slice-start
  323.4 10.2 copy-start.1
  339.9 10.2 copy-start
  353.3 9.0 slice-start
  376.6 10.2 copy-start.1
  393.1 10.2 copy-start
  406.5 9.0 slice-start
  429.8 10.2 copy-start.1
  446.3 10.2 copy-start
  459.7 9.0 slice-start
  483.1 10.2 copy-start.1
  499.5 10.2 copy-start
  512.9 9.0 slice-start
  536.3 10.2 copy-start.1
  552.7 10.2 copy-start
  566.2 9.0 slice-start
  589.5 10.2 copy-start.1
  605.9 10.2 copy-start
  619.4 9.0 slice-start
  642.7 10.2 copy-start.1
  659.1 10.2 copy-start
  672.6 9.0 slice-start
  695.9 10.2 copy-start.1
  712.3 10.2 copy-start
  725.8 9.0 slice-start
  749.1 10.2 copy-start.1
  765.6 10.2 copy-start
  779.0 9.0 slice-start
  780.1 7.9 slice-start.1
  802.3 10.2 copy-start.1
  818.8 10.2 copy-start
  832.2 9.0 slice-start
  833.3 7.9 slice-start.1
  855.5 10.2 copy-start.1
  872.0 10.2 copy-start
  885.4 9.0 slice-start
  886.5 7.9 slice-start.1
  899.9 50.9 %copy-start.4 = (f32[128,4096]{1,0:T(8,128)S(1)}, f32[128,4096]{1,0:T(8,128)}, u32[]{:S(2)}) copy-start(f32[128,4096]{1,0:T(8,128)} %get-tuple-element.241) | copy-start | bytes 6291460
  900.0 158.7 %all-reduce.3.cloned.1.call-start = ((), (), s32[]{:S(2)}) async-start(), calls=%async_computation.2 | async-start | bytes 2097152 | tf_op jit(solution)/shard_map/psum | solution.py:81
  (59 other events, 303.5 us)
Sparse Core Ops, SparseCore 0:
  900.1 12.3 reduce-scatter.1
  950.4 108.2 all-reduce.2
where the time goes:
time: 1080 us; the launch traced here: 1070 us
  local copies, waits for them, and re-layouts  672 us (62%)
  other arithmetic  207 us (19%)
  waiting for transfers between devices  107 us (10%)
  blocking collectives  47.4 us (4%)
  between operations  14.8 us (1%)
  loops' own time  12.5 us (1%)
    while x448, local copies, waits for them, and re-layouts  566 us
    reduce_sum x16, other arithmetic, one_block(): accum = accum + jnp.sum(weighted, axis=1)  117 us
    psum x1, waiting for transfers between devices, shards(): summed = lax.psum((taps_part, skip_part), 'dp')  107 us
    reduce_sum x16, other arithmetic, one_block(): return (accum, jnp.sum(masked, axis=0))  59.2 us
    another operation x16, local copies, waits for them, and re-layouts, one_block(): jnp.stack([lax.dynamic_slice_in_dim(u_ext, begin, rows, 0) for begin in l...  49 us
    psum x1, blocking collectives, shards(): summed = lax.psum((taps_part, skip_part), 'dp')  44 us
  transfers between devices with their start and end apart: 4, of which 1 were waited for; matrix products, arithmetic and copies ran while one was open for 1% of the time, Pallas kernels for 0%

commit v1 on v0

v1 whole, which is shorter than its diff:
```python
import functools
import jax
import jax.numpy as jnp
from jax import lax
from jax.experimental import pallas as pl
from jax.experimental.pallas import tpu as pltpu
from jax.sharding import PartitionSpec as P

LANES = 128
STEP = 8
GROUP = 4
SPAN = STEP * GROUP
DOCS = 4


def up(value, unit):
    return -(-value // unit) * unit


def documents(ids_ref, info_ref):
    ids = ids_ref[...]
    begin = jnp.int32(0)
    place = jnp.int32(0)
    for doc in range(DOCS):
        count = jnp.sum(jnp.where(ids == doc, 1.0, 0.0)).astype(jnp.int32)
        spans = (count + (SPAN - 1)) // SPAN
        info_ref[doc] = begin
        info_ref[DOCS + doc] = count
        info_ref[2 * DOCS + doc] = spans
        info_ref[3 * DOCS + doc] = place
        begin = begin + count
        place = place + (spans + 1) * SPAN


def widen(refs, shards, rows, full_ref):
    for ref, shard in zip(refs, shards):
        at = pl.multiple_of(shard * rows, STEP)
        full_ref[pl.ds(at, rows), :] = ref[...].reshape(rows, LANES).astype(jnp.float32)


def separate(info_ref, g_ref, docs_ref):
    sublane = lax.broadcasted_iota(jnp.int32, (STEP, LANES), 0)
    for doc in range(DOCS):
        begin = info_ref[doc]
        count = info_ref[DOCS + doc]
        spans = info_ref[2 * DOCS + doc]
        place = info_ref[3 * DOCS + doc]

        def move(span, _):
            for i in range(GROUP):
                row = span * SPAN + i * STEP
                tile = g_ref[pl.ds(begin + row, STEP), :]
                tile = jnp.where(sublane < count - row, tile, 0.0)
                docs_ref[pl.ds(pl.multiple_of(place + row, STEP), STEP), :] = tile
            return 0

        lax.fori_loop(0, spans, move, 0)
        docs_ref[pl.ds(pl.multiple_of(place + spans * SPAN, STEP), SPAN), :] = jnp.zeros(
            (SPAN, LANES), jnp.float32
        )


def sources(me, count):
    return [lax.rem(me - k + count, count) for k in range(count)]


def filter_kernel(shards, rows, scale, me_ref, *refs):
    u_refs = refs[:shards]
    g_refs = refs[shards : 2 * shards]
    ids_ref, out_ref, info_ref, u_full, g_full, g_docs, parts = refs[2 * shards :]
    length = shards * rows
    kernel = out_ref.shape[1]

    @pl.when(pl.program_id(0) == 0)
    def _():
        documents(ids_ref, info_ref)
        u_full[length:, :] = jnp.zeros((u_full.shape[0] - length, LANES), jnp.float32)

    order = sources(me_ref[0], shards)
    widen(u_refs, order, rows, u_full)
    widen(g_refs, order, rows, g_full)
    separate(info_ref, g_full, g_docs)

    def one_part(part, _):
        sums = [jnp.zeros((STEP, LANES), jnp.float32) for _ in range(SPAN)]

        def pairs(doc, whole, span, sums):
            sums = list(sums)
            at = info_ref[doc] + span * SPAN
            base = pl.multiple_of(info_ref[3 * DOCS + doc] + (span + part) * SPAN, SPAN)
            u = [u_full[pl.ds(at + i * STEP, STEP), :] for i in range(GROUP)]
            for q in range(STEP):
                tiles = 2 * GROUP - 1 if whole else GROUP
                g = [g_docs[pl.ds(base + m * STEP + q, STEP), :] for m in range(tiles)]
                for p in range(GROUP):
                    total = None
                    for i in range(GROUP if whole else GROUP - p):
                        term = u[i] * g[i + p]
                        total = term if total is None else total + term
                    sums[p * STEP + q] = sums[p * STEP + q] + total
            return tuple(sums)

        for doc in range(DOCS):
            last = info_ref[2 * DOCS + doc] - 1 - part
            sums = lax.fori_loop(0, jnp.maximum(last, 0), functools.partial(pairs, doc, True), tuple(sums))
            edge = jnp.maximum(last, 0)
            sums = lax.fori_loop(
                edge, jnp.where(last >= 0, edge + 1, edge), functools.partial(pairs, doc, False), tuple(sums)
            )
        for k in range(SPAN):
            at = pl.multiple_of((part * SPAN + k) * STEP, STEP)
            parts[pl.ds(at, STEP), :] = sums[k]
        return 0

    lax.fori_loop(0, kernel // SPAN, one_part, 0)
    columns = []
    for block in range(kernel // STEP):
        first = block * STEP * STEP
        total = parts[pl.ds(first, STEP, stride=STEP), :]
        for r in range(1, STEP):
            total = total + parts[pl.ds(first + r, STEP, stride=STEP), :]
        columns.append(total)
    out_ref[...] = jnp.concatenate(columns, axis=0).T * scale


def grad_kernel(shards, rows, me_ref, *refs):
    g_refs = refs[:shards]
    ids_ref, taps_ref, skip_ref = refs[shards : shards + 3]
    out_refs = refs[shards + 3 : 2 * shards + 3]
    info_ref, g_full, g_docs, taps_full, total_ref = refs[2 * shards + 3 :]
    length = shards * rows
    kernel = taps_ref.shape[1]

    @pl.when(pl.program_id(0) == 0)
    def _():
        documents(ids_ref, info_ref)

    order = sources(me_ref[0], shards)
    widen(g_refs, order, rows, g_full)
    separate(info_ref, g_full, g_docs)
    taps_full[...] = taps_ref[...].astype(jnp.float32).T
    total_ref[:length, :] = g_full[:length, :] * skip_ref[...]

    def one_part(part, _):
        taps = [taps_full[pl.ds(part * SPAN + k, STEP, stride=0), :] for k in range(SPAN)]

        def pairs(doc, whole, span, _):
            at = info_ref[doc] + span * SPAN
            base = pl.multiple_of(info_ref[3 * DOCS + doc] + (span + part) * SPAN, SPAN)
            total = [total_ref[pl.ds(at + i * STEP, STEP), :] for i in range(GROUP)]
            for q in range(STEP):
                tiles = 2 * GROUP - 1 if whole else GROUP
                g = [g_docs[pl.ds(base + m * STEP + q, STEP), :] for m in range(tiles)]
                for p in range(GROUP):
                    for i in range(GROUP if whole else GROUP - p):
                        total[i] = total[i] + taps[p * STEP + q] * g[i + p]
            for i in range(GROUP):
                total_ref[pl.ds(at + i * STEP, STEP), :] = total[i]
            return 0

        for doc in range(DOCS):
            last = info_ref[2 * DOCS + doc] - 1 - part
            edge = jnp.maximum(last, 0)
            lax.fori_loop(0, edge, functools.partial(pairs, doc, True), 0)
            lax.fori_loop(edge, jnp.where(last >= 0, edge + 1, edge), functools.partial(pairs, doc, False), 0)
        return 0

    lax.fori_loop(0, kernel // SPAN, one_part, 0)
    for out_ref, shard in zip(out_refs, order):
        at = pl.multiple_of(shard * rows, STEP)
        out_ref[...] = total_ref[pl.ds(at, rows), :].astype(out_ref.dtype).reshape(out_ref.shape)


def sizes(shards, rows):
    length = shards * rows
    docs_rows = up(length, SPAN) + 2 * DOCS * SPAN
    return length + SPAN, docs_rows


def filter_part(me, u_list, g_list, ids, kernel, scale, width, first, count):
    shards = len(u_list)
    rows = u_list[0].shape[1]
    blocks = width // LANES
    tall, docs_rows = sizes(shards, rows)
    data = pl.BlockSpec((1, rows, LANES), lambda c, me_ref: (0, 0, me_ref[0] * blocks + first + c))
    pairs = 5 * rows * shards * kernel * count * LANES // 16
    return pl.pallas_call(
        functools.partial(filter_kernel, shards, rows, scale),
        out_shape=jax.ShapeDtypeStruct((count * LANES, kernel), jnp.float32),
        grid_spec=pltpu.PrefetchScalarGridSpec(
            num_scalar_prefetch=1,
            grid=(count,),
            in_specs=[data] * (2 * shards) + [pl.BlockSpec(ids.shape, lambda c, me_ref: (0, 0))],
            out_specs=pl.BlockSpec((LANES, kernel), lambda c, me_ref: (c, 0)),
            scratch_shapes=[
                pltpu.SMEM((4 * DOCS,), jnp.int32),
                pltpu.VMEM((tall, LANES), jnp.float32),
                pltpu.VMEM((tall, LANES), jnp.float32),
                pltpu.VMEM((docs_rows, LANES), jnp.float32),
                pltpu.VMEM((kernel * STEP, LANES), jnp.float32),
            ],
        ),
        cost_estimate=pl.CostEstimate(
            flops=2 * pairs, bytes_accessed=count * LANES * (4 * rows * shards + 4 * kernel), transcendentals=0
        ),
    )(me, *u_list, *g_list, ids)


def grad_part(me, g_list, ids, taps, skip_gain, width):
    shards = len(g_list)
    rows = g_list[0].shape[1]
    kernel = taps.shape[1]
    blocks = width // LANES
    tall, docs_rows = sizes(shards, rows)
    data = pl.BlockSpec((1, rows, LANES), lambda c, me_ref: (0, 0, me_ref[0] * blocks + c))
    pairs = 5 * rows * shards * kernel * width // 16
    return pl.pallas_call(
        functools.partial(grad_kernel, shards, rows),
        out_shape=[jax.ShapeDtypeStruct((1, rows, width), jnp.bfloat16)] * shards,
        grid_spec=pltpu.PrefetchScalarGridSpec(
            num_scalar_prefetch=1,
            grid=(blocks,),
            in_specs=[data] * shards
            + [
                pl.BlockSpec(ids.shape, lambda c, me_ref: (0, 0)),
                pl.BlockSpec((LANES, kernel), lambda c, me_ref: (me_ref[0] * blocks + c, 0)),
                pl.BlockSpec((1, LANES), lambda c, me_ref: (0, me_ref[0] * blocks + c)),
            ],
            out_specs=[pl.BlockSpec((1, rows, LANES), lambda c, me_ref: (0, 0, c))] * shards,
            scratch_shapes=[
                pltpu.SMEM((4 * DOCS,), jnp.int32),
                pltpu.VMEM((tall, LANES), jnp.float32),
                pltpu.VMEM((docs_rows, LANES), jnp.float32),
                pltpu.VMEM((kernel, LANES), jnp.float32),
                pltpu.VMEM((tall, LANES), jnp.float32),
            ],
        ),
        cost_estimate=pl.CostEstimate(
            flops=2 * pairs, bytes_accessed=width * (4 * rows * shards + 2 * kernel), transcendentals=0
        ),
    )(me, *g_list, ids, taps, skip_gain.reshape(1, -1))


CHUNKS = 2


def shifted(array, axis, count, step):
    return lax.ppermute(array, axis, [(i, (i + step) % count) for i in range(count)])


def reduced(part, axis, count):
    rows = up(part.shape[0], count)
    part = jnp.pad(part, ((0, rows - part.shape[0]), (0, 0)))
    pieces = lax.all_to_all(part.reshape(count, rows // count, -1), axis, 0, 0, tiled=True)
    return jnp.sum(pieces, axis=0)


def gathered(piece, axis, count, rows):
    copies = jnp.broadcast_to(piece[None], (count,) + piece.shape)
    return lax.all_to_all(copies, axis, 0, 0, tiled=True).reshape(-1, piece.shape[1])[:rows]


def shards(inputs, cotangent, segment_ids, taps, skip_gain):
    count = lax.axis_size("ctx")
    groups = lax.axis_size("dp")
    me = lax.axis_index("ctx").astype(jnp.int32)[None]
    width = inputs.shape[2] // count
    scale = 1.0 / (inputs.shape[0] * groups)
    u_list = [inputs] + [shifted(inputs, "ctx", count, k) for k in range(1, count)]
    g_list = [cotangent] + [shifted(cotangent, "ctx", count, k) for k in range(1, count)]
    blocks = width // LANES
    each = blocks // CHUNKS
    kernel = taps.shape[1]
    shares = []
    for chunk in range(CHUNKS):
        part = filter_part(me, u_list, g_list, segment_ids, kernel, scale, width, chunk * each, each)
        shares.append(reduced(part, "dp", groups))
    parts = grad_part(me, g_list, segment_ids, taps, skip_gain, width)
    whole = [gathered(share, "dp", groups, each * LANES) for share in shares]
    taps_grad = jnp.concatenate(whole, axis=0)
    input_grad = jnp.zeros(inputs.shape, jnp.bfloat16)
    for k in range(count):
        got = parts[k] if k == 0 else shifted(parts[k], "ctx", count, -k)
        owner = lax.rem(me[0] + k, count) if k else me[0]
        input_grad = lax.dynamic_update_slice(input_grad, got, (0, 0, owner * width))
    return input_grad, taps_grad, taps_grad[:, 0]


def solution(mesh):
    return jax.shard_map(
        shards,
        mesh=mesh,
        in_specs=(P("dp", "ctx", None), P("dp", "ctx", None), P("dp", None), P(), P()),
        out_specs=(P("dp", "ctx", None), P("ctx", None), P("ctx")),
        check_vma=False,
    )
```

time: 1080 us -> 112 us (0.10); the launches traced: 1070 us -> 111 us
  local copies, waits for them, and re-layouts: 672 us -> 3.78 us
  other arithmetic: 207 us -> 2.06 us
  waiting for transfers between devices: 107 us -> 37.5 us
  blocking collectives: 47.4 us -> 0 us
  Pallas kernels: 0 us -> 45.9 us
  between operations: 14.8 us -> 0.74 us
  starting transfers between devices: 7.16 us -> 21.1 us
  loops' own time: 12.5 us -> 0 us
    while x448 -> x0, local copies, waits for them, and re-layouts: 566 us -> none
    reduce_sum x32 -> x2, other arithmetic: 176 us -> 0.07 us  [reduced(): return jnp.sum(pieces, axis=0)]
    psum x1 -> x0, waiting for transfers between devices: 107 us -> none  [shards(): summed = lax.psum((taps_part, skip_part), 'dp')]
    another operation x65 -> x0, local copies, waits for them, and re-layouts: 51.7 us -> none  [the longest x16 49 us: one_block(): jnp.stack([lax.dynamic_slice_in_dim(u_ext, begin, rows, 0) for begin in l...]
    pallas_call x0 -> x3, Pallas kernels: none -> 45.9 us  [the longest x2 23.6 us: filter_part(): pl.pallas_call(functools.partial(filter_kernel, shards, rows, scale), out...]
    psum x1 -> x0, blocking collectives: 44 us -> none  [shards(): summed = lax.psum((taps_part, skip_part), 'dp')]
    all_to_all x0 -> x4, waiting for transfers between devices: none -> 32.6 us  [the longest x2 18.2 us: reduced(): lax.all_to_all(part.reshape(count, rows // count, -1), axis, 0, 0, tiled=...]
    all_to_all x0 -> x4, starting transfers between devices: none -> 20.4 us  [the longest x2 12.6 us: reduced(): lax.all_to_all(part.reshape(count, rows // count, -1), axis, 0, 0, tiled=...]
  transfers between devices with their start and end apart: 4 -> 7, of which waited for: 1 -> 6; matrix products, arithmetic and copies ran while one was open for 1% -> 0% of each run, Pallas kernels for 0% -> 31%
where the time goes in v1:
time: 112 us; the launch traced here: 111 us
  Pallas kernels  45.9 us (41%)
  waiting for transfers between devices  37.5 us (33%)
  starting transfers between devices  21.1 us (19%)
  local copies, waits for them, and re-layouts  3.78 us (3%)
  other arithmetic  2.06 us (2%)
    pallas_call x2, Pallas kernels, filter_part(): pl.pallas_call(functools.partial(filter_kernel, shards, rows, scale), out...  23.6 us
    pallas_call x1, Pallas kernels, grad_part(): pl.pallas_call(functools.partial(grad_kernel, shards, rows), out_shape=[j...  22.3 us
    all_to_all x2, waiting for transfers between devices, reduced(): lax.all_to_all(part.reshape(count, rows // count, -1), axis, 0, 0, tiled=...  18.2 us
    all_to_all x2, waiting for transfers between devices, gathered(): lax.all_to_all(copies, axis, 0, 0, tiled=True).reshape(-1, piece.shape[1])  14.4 us
    all_to_all x2, starting transfers between devices, reduced(): lax.all_to_all(part.reshape(count, rows // count, -1), axis, 0, 0, tiled=...  12.6 us
    all_to_all x2, starting transfers between devices, gathered(): lax.all_to_all(copies, axis, 0, 0, tiled=True).reshape(-1, piece.shape[1])  7.83 us
    ppermute x3, waiting for transfers between devices, shifted(): lax.ppermute(array, axis, [(i, (i + step) % count) for i in range(count)])  4.92 us
  transfers between devices with their start and end apart: 7, of which 6 were waited for; matrix products, arithmetic and copies ran while one was open for 0% of the time, Pallas kernels for 31%

profile of v1, /device:TPU:0, one launch (start us, length us, event | category | flops | bytes accessed | tf_op | source)
XLA Modules:
  0.0 111.1 jit_solution(6241054787350040775)
XLA Ops:
  0.6 0.6 collective-permute-start.2
  1.2 0.1 collective-permute-start
  1.3 2.4 %collective-permute-done.2.refs_1_ = bf16[1,128,4096]{2,1,0:T(8,128)(2,1)S(1)} collective-permute-done((bf16[1,128,4096]{2,1,0:T(8,128)(2,1)}, bf16[1,128,4096]{2,1,0:T(8,128)(2,1)S(1)}, u32[]{:S(2)}, u32[]{:S(2)}) %collective-permute-start.2) | collective-permute-done | bytes 1048608 | tf_op jit(solution)/shard_map/ppermute | solution.py:248
  3.7 0.0 copy-start.1
  3.7 1.5 %collective-permute-done.refs_1_.refs_3_ = bf16[1,128,4096]{2,1,0:T(8,128)(2,1)S(1)} collective-permute-done((bf16[1,128,4096]{2,1,0:T(8,128)(2,1)}, bf16[1,128,4096]{2,1,0:T(8,128)(2,1)S(1)}, u32[]{:S(2)}, u32[]{:S(2)}) %collective-permute-start) | collective-permute-done | bytes 1048608 | tf_op jit(solution)/shard_map/ppermute | solution.py:248
  5.2 0.0 copy-start
  5.2 0.0 copy-done.1
  5.2 1.0 copy-done
  6.2 11.8 %shard_map.77 = f32[1024,128]{1,0:T(8,128)} custom-call(s32[1]{0:T(128)} %bitcast.me_ref, bf16[1,128,4096]{2,1,0:T(8,128)(2,1)} %refs_0_.5, bf16[1,128,4096]{2,1,0:T(8,128)(2,1)} %copy-done.1, bf16[1,128,4096]{2,1,0:T(8,128)(2,1)} %refs_2_.5, bf16[1,128,4096]{2,1,0:T(8,128)(2,1)} %copy-done, s32[1,256]{1,0:T(1,128)} %refs_4_.3), custom_call_target="tpu_custom_call" | custom-call | flops 20971520 | bytes 1572864 | tf_op jit(solution)/shard_map/pallas_call | solution.py:187
  17.9 8.7 %all-to-all-start = ((f32[16,64,128]{2,1,0:T(8,128)}), f32[16,64,128]{2,1,0:T(8,128)S(1)}, u32[]{:S(2)}, u32[]{:S(2)}) async-start(f32[16,64,128]{2,1,0:T(8,128)} %bitcast.11), calls=%async_computation | async-start | bytes 1048576 | tf_op jit(solution)/shard_map/all_to_all | solution.py:254
  26.6 11.8 %shard_map.78 = f32[1024,128]{1,0:T(8,128)} custom-call(s32[1]{0:T(128)} %bitcast.me_ref, bf16[1,128,4096]{2,1,0:T(8,128)(2,1)} %refs_0_.5, bf16[1,128,4096]{2,1,0:T(8,128)(2,1)} %copy-done.1, bf16[1,128,4096]{2,1,0:T(8,128)(2,1)} %refs_2_.5, bf16[1,128,4096]{2,1,0:T(8,128)(2,1)} %copy-done, s32[1,256]{1,0:T(1,128)} %refs_4_.3), custom_call_target="tpu_custom_call" | custom-call | flops 20971520 | bytes 1572864 | tf_op jit(solution)/shard_map/pallas_call | solution.py:187
  38.4 3.6 %all-to-all-done = f32[16,64,128]{2,1,0:T(8,128)S(1)} async-done(((f32[16,64,128]{2,1,0:T(8,128)}), f32[16,64,128]{2,1,0:T(8,128)S(1)}, u32[]{:S(2)}, u32[]{:S(2)}) %all-to-all-start) | async-done | bytes 524320 | tf_op jit(solution)/shard_map/all_to_all | solution.py:254
  42.0 3.9 %all-to-all-start.2 = ((f32[16,64,128]{2,1,0:T(8,128)}), f32[16,64,128]{2,1,0:T(8,128)S(1)}, u32[]{:S(2)}, u32[]{:S(2)}) async-start(f32[16,64,128]{2,1,0:T(8,128)} %bitcast.10), calls=%async_computation.2 | async-start | bytes 1048576 | tf_op jit(solution)/shard_map/all_to_all | solution.py:254
  46.0 14.6 %all-to-all-done.2 = f32[16,64,128]{2,1,0:T(8,128)S(1)} async-done(((f32[16,64,128]{2,1,0:T(8,128)}), f32[16,64,128]{2,1,0:T(8,128)S(1)}, u32[]{:S(2)}, u32[]{:S(2)}) %all-to-all-start.2) | async-done | bytes 524320 | tf_op jit(solution)/shard_map/all_to_all | solution.py:254
  60.6 0.8 broadcast_in_dim.20
  61.5 3.9 %all-to-all-start.1 = ((f32[16,64,128]{2,1,0:T(8,128)}), f32[16,64,128]{2,1,0:T(8,128)S(1)}, u32[]{:S(2)}, u32[]{:S(2)}) async-start(f32[16,64,128]{2,1,0:T(8,128)} %broadcast_in_dim.20), calls=%async_computation.1 | async-start | bytes 1048576 | tf_op jit(solution)/shard_map/all_to_all | solution.py:260
  65.5 14.4 %all-to-all-done.1 = f32[16,64,128]{2,1,0:T(8,128)S(1)} async-done(((f32[16,64,128]{2,1,0:T(8,128)}), f32[16,64,128]{2,1,0:T(8,128)S(1)}, u32[]{:S(2)}, u32[]{:S(2)}) %all-to-all-start.1) | async-done | bytes 524320 | tf_op jit(solution)/shard_map/all_to_all | solution.py:260
  79.8 0.8 broadcast_in_dim.21
  80.7 3.9 %all-to-all-start.3 = ((f32[16,64,128]{2,1,0:T(8,128)}), f32[16,64,128]{2,1,0:T(8,128)S(1)}, u32[]{:S(2)}, u32[]{:S(2)}) async-start(f32[16,64,128]{2,1,0:T(8,128)} %broadcast_in_dim.21), calls=%async_computation.3 | async-start | bytes 1048576 | tf_op jit(solution)/shard_map/all_to_all | solution.py:260
  84.6 22.3 %shard_map.76 = (bf16[1,128,2048]{2,1,0:T(8,128)(2,1)}, bf16[1,128,2048]{2,1,0:T(8,128)(2,1)}) custom-call(s32[1]{0:T(128)} %bitcast.me_ref, bf16[1,128,4096]{2,1,0:T(8,128)(2,1)} %refs_2_.5, bf16[1,128,4096]{2,1,0:T(8,128)(2,1)} %copy-done, s32[1,256]{1,0:T(1,128)} %refs_4_.3, bf16[4096,128]{1,0:T(8,128)(2,1)} %refs_3_.1, f32[1,4096]{1,0:T(1,128)} %bitcast.12), custom_call_target="tpu_custom_call" | custom-call | flops 41943040 | bytes 2621440 | tf_op jit(solution)/shard_map/pallas_call | solution.py:217
  106.9 0.0 collective-permute-start.1
  106.9 0.0 copy-start.3
  106.9 0.1 broadcast_in_dim.8
  107.0 0.9 copy-done.3
  108.0 1.0 collective-permute-done.1
  109.1 0.0 copy-start.2
  109.1 0.0 all-to-all-done.3
  109.1 0.9 fusion.1
  110.0 1.0 pad_maximum_fusion
  111.1 0.0 copy-done.2
  (4 shorter events, 0.2 us)
Async XLA Ops:
  0.6 3.1 %collective-permute-start.2 = (bf16[1,128,4096]{2,1,0:T(8,128)(2,1)}, bf16[1,128,4096]{2,1,0:T(8,128)(2,1)S(1)}, u32[]{:S(2)}, u32[]{:S(2)}) collective-permute-start(bf16[1,128,4096]{2,1,0:T(8,128)(2,1)} %refs_0_.5), channel_id=1, source_target_pairs={{0,1},{1,0},{2,3},{3,2},{4,5},{5,4},{6,7},{7,6},{8,9},{9,8},{10,11... | collective-permute-start | bytes 3145736 | tf_op jit(solution)/shard_map/ppermute | solution.py:248
  1.2 4.0 %collective-permute-start = (bf16[1,128,4096]{2,1,0:T(8,128)(2,1)}, bf16[1,128,4096]{2,1,0:T(8,128)(2,1)S(1)}, u32[]{:S(2)}, u32[]{:S(2)}) collective-permute-start(bf16[1,128,4096]{2,1,0:T(8,128)(2,1)} %refs_2_.5), channel_id=1, source_target_pairs={{0,1},{1,0},{2,3},{3,2},{4,5},{5,4},{6,7},{7,6},{8,9},{9,8},{10,11... | collective-permute-start | bytes 3145736 | tf_op jit(solution)/shard_map/ppermute | solution.py:248
  3.7 1.5 %copy-start.1 = (bf16[1,128,4096]{2,1,0:T(8,128)(2,1)}, bf16[1,128,4096]{2,1,0:T(8,128)(2,1)S(1)}, u32[]{:S(2)}) copy-start(bf16[1,128,4096]{2,1,0:T(8,128)(2,1)S(1)} %collective-permute-done.2.refs_1_) | copy-start | bytes 3145732
  5.2 1.0 copy-start
  17.9 24.1 %all-to-all-start = ((f32[16,64,128]{2,1,0:T(8,128)}), f32[16,64,128]{2,1,0:T(8,128)S(1)}, u32[]{:S(2)}, u32[]{:S(2)}) async-start(f32[16,64,128]{2,1,0:T(8,128)} %bitcast.11), calls=%async_computation | async-start | bytes 1048576 | tf_op jit(solution)/shard_map/all_to_all | solution.py:254
  42.0 18.6 %all-to-all-start.2 = ((f32[16,64,128]{2,1,0:T(8,128)}), f32[16,64,128]{2,1,0:T(8,128)S(1)}, u32[]{:S(2)}, u32[]{:S(2)}) async-start(f32[16,64,128]{2,1,0:T(8,128)} %bitcast.10), calls=%async_computation.2 | async-start | bytes 1048576 | tf_op jit(solution)/shard_map/all_to_all | solution.py:254
  61.5 18.4 %all-to-all-start.1 = ((f32[16,64,128]{2,1,0:T(8,128)}), f32[16,64,128]{2,1,0:T(8,128)S(1)}, u32[]{:S(2)}, u32[]{:S(2)}) async-start(f32[16,64,128]{2,1,0:T(8,128)} %broadcast_in_dim.20), calls=%async_computation.1 | async-start | bytes 1048576 | tf_op jit(solution)/shard_map/all_to_all | solution.py:260
  80.7 28.4 %all-to-all-start.3 = ((f32[16,64,128]{2,1,0:T(8,128)}), f32[16,64,128]{2,1,0:T(8,128)S(1)}, u32[]{:S(2)}, u32[]{:S(2)}) async-start(f32[16,64,128]{2,1,0:T(8,128)} %broadcast_in_dim.21), calls=%async_computation.3 | async-start | bytes 1048576 | tf_op jit(solution)/shard_map/all_to_all | solution.py:260
  106.9 2.1 %collective-permute-start.1 = (bf16[1,128,2048]{2,1,0:T(8,128)(2,1)}, bf16[1,128,2048]{2,1,0:T(8,128)(2,1)S(1)}, u32[]{:S(2)}, u32[]{:S(2)}) collective-permute-start(bf16[1,128,2048]{2,1,0:T(8,128)(2,1)} %get-tuple-element.6), channel_id=1, source_target_pairs={{0,1},{1,0},{2,3},{3,2},{4,5},{5,4},{6,7},{7,6},{8,9},{9,8},{10,11... | collective-permute-start | bytes 1572872 | tf_op jit(solution)/shard_map/ppermute | solution.py:248
  106.9 1.0 copy-start.3
  109.1 2.0 %copy-start.2 = (bf16[1,128,4096]{2,1,0:T(8,128)(2,1)}, bf16[1,128,4096]{2,1,0:T(8,128)(2,1)S(1)}, u32[]{:S(2)}) copy-start(bf16[1,128,4096]{2,1,0:T(8,128)(2,1)S(1)} %constant_dynamic-update-slice_fusion) | copy-start | bytes 3145732

commit v2 on v1

v2 whole, which is shorter than its diff:
```python
import functools
import math
import jax
import jax.numpy as jnp
import numpy as np
from jax import lax
from jax.experimental import pallas as pl
from jax.experimental.pallas import tpu as pltpu
from jax.sharding import PartitionSpec as P

LANES = 128
STEP = 8
TILES = 2
BLOCK = LANES * TILES
DOCS = 4


def up(value, unit):
    return -(-value // unit) * unit


def halves(table):
    high = np.asarray(table, np.float32).astype(jnp.bfloat16)
    low = (np.asarray(table, np.float64) - high.astype(np.float64)).astype(np.float32).astype(jnp.bfloat16)
    return high, low


def tables(most, kernel):
    period = most + kernel
    waves = period // 2
    angle = np.pi * np.outer(2 * np.arange(waves) + 1, np.arange(most)) / period
    ahead = halves(np.concatenate([np.cos(angle), -np.sin(angle)], axis=0))
    back = halves(np.concatenate([np.cos(angle), -np.sin(angle)], axis=0).T / waves)
    ahead = np.concatenate(ahead, axis=1)
    back = np.concatenate([back[0], back[0], back[1]], axis=1)
    return ahead, back


def spectrum(table, value):
    return jnp.dot(table, jnp.concatenate([value, value], axis=0), preferred_element_type=jnp.float32)


def against(left, right):
    waves = left.shape[0] // 2
    lr, li = left[:waves], left[waves:]
    rr, ri = right[:waves], right[waves:]
    return lr * rr + li * ri, li * rr - lr * ri


def inverse(table, real, imag):
    value = jnp.concatenate([real, imag], axis=0)
    high = value.astype(jnp.bfloat16)
    low = (value - high.astype(jnp.float32)).astype(jnp.bfloat16)
    return jnp.dot(table, jnp.concatenate([high, low, high], axis=0), preferred_element_type=jnp.float32)


def documents(ids_ref, info_ref):
    ids = ids_ref[...]
    begin = jnp.int32(0)
    for doc in range(DOCS):
        count = jnp.sum(jnp.where(ids == doc, 1.0, 0.0)).astype(jnp.int32)
        info_ref[doc] = begin
        info_ref[DOCS + doc] = count
        begin = begin + count


def widen(refs, shards, rows, full_ref):
    for ref, shard in zip(refs, shards):
        at = pl.multiple_of(shard * rows, STEP)
        for tile in range(TILES):
            block = ref[0, :, tile * LANES : (tile + 1) * LANES]
            full_ref[tile, pl.ds(at, rows), :] = block.astype(jnp.float32)


def window(full_ref, begin, most, count=None):
    tiles = []
    for tile in range(TILES):
        column = [full_ref[tile, pl.ds(begin + i, STEP), :] for i in range(0, most, STEP)]
        tiles.append(jnp.concatenate(column, axis=0))
    value = jnp.concatenate(tiles, axis=1)
    if count is not None:
        value = jnp.where(lax.broadcasted_iota(jnp.int32, value.shape, 0) < count, value, 0.0)
    return value.astype(jnp.bfloat16)


def sources(me, count):
    return [lax.rem(me - k + count, count) for k in range(count)]


def filter_kernel(shards, rows, most, scale, me_ref, *refs):
    u_refs = refs[:shards]
    g_refs = refs[shards : 2 * shards]
    ids_ref, ahead_ref, back_ref, out_ref, info_ref, u_full, g_full = refs[2 * shards :]
    length = shards * rows
    kernel = out_ref.shape[1]

    @pl.when(pl.program_id(0) == 0)
    def _():
        documents(ids_ref, info_ref)
        u_full[:, length:, :] = jnp.zeros((TILES, most, LANES), jnp.float32)

    order = sources(me_ref[0], shards)
    widen(u_refs, order, rows, u_full)
    widen(g_refs, order, rows, g_full)
    ahead = ahead_ref[...]
    real, imag = 0.0, 0.0
    for doc in range(DOCS):
        begin = info_ref[doc]
        g_wave = spectrum(ahead, window(g_full, begin, most, info_ref[DOCS + doc]))
        u_wave = spectrum(ahead, window(u_full, begin, most))
        add_real, add_imag = against(g_wave, u_wave)
        real, imag = real + add_real, imag + add_imag
    taps = inverse(back_ref[:kernel, :], real, imag) * scale
    for tile in range(TILES):
        at = tile * LANES
        out_ref[at : at + LANES, :] = taps[:, at : at + LANES].T


def grad_kernel(shards, rows, most, me_ref, *refs):
    g_refs = refs[:shards]
    ids_ref, ahead_ref, head_ref, back_ref, taps_ref, skip_ref = refs[shards : shards + 6]
    out_refs = refs[shards + 6 : 2 * shards + 6]
    info_ref, g_full, total_ref = refs[2 * shards + 6 :]

    @pl.when(pl.program_id(0) == 0)
    def _():
        documents(ids_ref, info_ref)

    order = sources(me_ref[0], shards)
    widen(g_refs, order, rows, g_full)
    ahead = ahead_ref[...]
    taps = taps_ref[...]
    h_wave = lax.dot_general(
        head_ref[...],
        jnp.concatenate([taps, taps], axis=1),
        (((1,), (1,)), ((), ())),
        preferred_element_type=jnp.float32,
    )
    for doc in range(DOCS):
        begin = info_ref[doc]
        g_wave = spectrum(ahead, window(g_full, begin, most, info_ref[DOCS + doc]))
        total = inverse(back_ref[...], *against(g_wave, h_wave))
        for tile in range(TILES):
            for i in range(0, most, STEP):
                total_ref[tile, pl.ds(begin + i, STEP), :] = total[i : i + STEP, tile * LANES : (tile + 1) * LANES]
    for out_ref, shard in zip(out_refs, order):
        at = pl.multiple_of(shard * rows, STEP)
        for tile in range(TILES):
            lanes = slice(tile * LANES, (tile + 1) * LANES)
            skipped = g_full[tile, pl.ds(at, rows), :] * skip_ref[:, lanes]
            out_ref[0, :, lanes] = (total_ref[tile, pl.ds(at, rows), :] + skipped).astype(out_ref.dtype)


def filter_part(me, u_list, g_list, ids, kernel, scale, width, first, count):
    shards = len(u_list)
    rows = u_list[0].shape[1]
    length = shards * rows
    most = length // 2
    blocks = width // BLOCK
    ahead, back = tables(most, kernel)
    data = pl.BlockSpec((1, rows, BLOCK), lambda c, me_ref: (0, 0, me_ref[0] * blocks + first + c))
    fixed = lambda array: pl.BlockSpec(array.shape, lambda c, me_ref: (0, 0))
    return pl.pallas_call(
        functools.partial(filter_kernel, shards, rows, most, scale),
        out_shape=jax.ShapeDtypeStruct((count * BLOCK, kernel), jnp.float32),
        grid_spec=pltpu.PrefetchScalarGridSpec(
            num_scalar_prefetch=1,
            grid=(count,),
            in_specs=[data] * (2 * shards) + [fixed(ids), fixed(ahead), fixed(back)],
            out_specs=pl.BlockSpec((BLOCK, kernel), lambda c, me_ref: (c, 0)),
            scratch_shapes=[
                pltpu.SMEM((2 * DOCS,), jnp.int32),
                pltpu.VMEM((TILES, length + most, LANES), jnp.float32),
                pltpu.VMEM((TILES, length + most, LANES), jnp.float32),
            ],
        ),
        cost_estimate=pl.CostEstimate(
            flops=2 * count * BLOCK * (2 * DOCS * ahead.size + kernel * back.shape[1]),
            bytes_accessed=count * BLOCK * (4 * length + 4 * kernel),
            transcendentals=0,
        ),
    )(me, *u_list, *g_list, ids, jnp.asarray(ahead), jnp.asarray(back))


def grad_part(me, g_list, ids, taps, skip_gain, width, first, count):
    shards = len(g_list)
    rows = g_list[0].shape[1]
    kernel = taps.shape[1]
    length = shards * rows
    most = length // 2
    blocks = width // BLOCK
    ahead, back = tables(most, kernel)
    head = np.concatenate([ahead[:, :kernel], ahead[:, most : most + kernel]], axis=1)
    data = pl.BlockSpec((1, rows, BLOCK), lambda c, me_ref: (0, 0, me_ref[0] * blocks + first + c))
    fixed = lambda array: pl.BlockSpec(array.shape, lambda c, me_ref: (0, 0))
    return pl.pallas_call(
        functools.partial(grad_kernel, shards, rows, most),
        out_shape=[jax.ShapeDtypeStruct((1, rows, count * BLOCK), jnp.bfloat16)] * shards,
        grid_spec=pltpu.PrefetchScalarGridSpec(
            num_scalar_prefetch=1,
            grid=(count,),
            in_specs=[data] * shards
            + [fixed(ids), fixed(ahead), fixed(head), fixed(back)]
            + [
                pl.BlockSpec((BLOCK, kernel), lambda c, me_ref: (me_ref[0] * blocks + first + c, 0)),
                pl.BlockSpec((1, BLOCK), lambda c, me_ref: (0, me_ref[0] * blocks + first + c)),
            ],
            out_specs=[pl.BlockSpec((1, rows, BLOCK), lambda c, me_ref: (0, 0, c))] * shards,
            scratch_shapes=[
                pltpu.SMEM((2 * DOCS,), jnp.int32),
                pltpu.VMEM((TILES, length + most, LANES), jnp.float32),
                pltpu.VMEM((TILES, length + most, LANES), jnp.float32),
            ],
        ),
        cost_estimate=pl.CostEstimate(
            flops=2 * count * BLOCK * (DOCS * (ahead.size + back.size) + head.size),
            bytes_accessed=count * BLOCK * (4 * length + 2 * kernel),
            transcendentals=0,
        ),
    )(me, *g_list, ids, jnp.asarray(ahead), jnp.asarray(head), jnp.asarray(back), taps, skip_gain.reshape(1, -1))


CHUNKS = 1


def shifted(array, axis, count, step):
    return lax.ppermute(array, axis, [(i, (i + step) % count) for i in range(count)])


def reduced(part, axis, count):
    rows = up(part.shape[0], count)
    part = jnp.pad(part, ((0, rows - part.shape[0]), (0, 0)))
    pieces = lax.all_to_all(part.reshape(count, rows // count, -1), axis, 0, 0, tiled=True)
    return jnp.sum(pieces, axis=0)


def gathered(piece, axis, count, rows):
    copies = jnp.broadcast_to(piece[None], (count,) + piece.shape)
    return lax.all_to_all(copies, axis, 0, 0, tiled=True).reshape(-1, piece.shape[1])[:rows]


def shards(inputs, cotangent, segment_ids, taps, skip_gain):
    count = lax.axis_size("ctx")
    groups = lax.axis_size("dp")
    me = lax.axis_index("ctx").astype(jnp.int32)[None]
    width = inputs.shape[2] // count
    scale = 1.0 / (inputs.shape[0] * groups)
    u_list = [inputs] + [shifted(inputs, "ctx", count, k) for k in range(1, count)]
    g_list = [cotangent] + [shifted(cotangent, "ctx", count, k) for k in range(1, count)]
    blocks = width // BLOCK
    each = blocks // CHUNKS
    kernel = taps.shape[1]
    shares = []
    for chunk in range(CHUNKS):
        part = filter_part(me, u_list, g_list, segment_ids, kernel, scale, width, chunk * each, each)
        shares.append(reduced(part, "dp", groups))
    parts = grad_part(me, g_list, segment_ids, taps, skip_gain, width, 0, blocks)
    whole = [gathered(share, "dp", groups, each * BLOCK) for share in shares]
    taps_grad = jnp.concatenate(whole, axis=0)
    input_grad = jnp.zeros(inputs.shape, jnp.bfloat16)
    for k in range(count):
        got = parts[k] if k == 0 else shifted(parts[k], "ctx", count, -k)
        owner = lax.rem(me[0] + k, count) if k else me[0]
        input_grad = lax.dynamic_update_slice(input_grad, got, (0, 0, owner * width))
    return input_grad, taps_grad, taps_grad[:, 0]


def solution(mesh):
    return jax.shard_map(
        shards,
        mesh=mesh,
        in_specs=(P("dp", "ctx", None), P("dp", "ctx", None), P("dp", None), P(), P()),
        out_specs=(P("dp", "ctx", None), P("ctx", None), P("ctx")),
        check_vma=False,
    )
```

time: 112 us -> 81.8 us (0.73)
  blocking collectives: 0 us -> 34.8 us
  Pallas kernels: 45.9 us -> 20 us
  waiting for transfers between devices: 37.5 us -> 15.7 us
  starting transfers between devices: 21.1 us -> 4.59 us
  other arithmetic: 2.06 us -> 0.06 us
  local copies, waits for them, and re-layouts: 3.78 us -> 5.08 us
    all_to_all x0 -> x1, blocking collectives: none -> 34.8 us  [reduced(): lax.all_to_all(part.reshape(count, rows // count, -1), axis, 0, 0, tiled=...]
    pallas_call x3 -> x2, Pallas kernels: 45.9 us -> 20 us  [the longest x1 10.7 us: grad_part(): pl.pallas_call(functools.partial(grad_kernel, shards, rows, most), out_sh...]
    all_to_all x2 -> x0, waiting for transfers between devices: 18.2 us -> none  [reduced(): lax.all_to_all(part.reshape(count, rows // count, -1), axis, 0, 0, tiled=...]
    all_to_all x2 -> x0, starting transfers between devices: 12.6 us -> none  [reduced(): lax.all_to_all(part.reshape(count, rows // count, -1), axis, 0, 0, tiled=...]
    all_to_all x2 -> x1, starting transfers between devices: 7.83 us -> 3.95 us  [gathered(): lax.all_to_all(copies, axis, 0, 0, tiled=True).reshape(-1, piece.shape[1])]
    all_to_all x2 -> x1, waiting for transfers between devices: 14.4 us -> 10.7 us  [gathered(): lax.all_to_all(copies, axis, 0, 0, tiled=True).reshape(-1, piece.shape[1])]
    unnamed x8 -> x9, local copies, waits for them, and re-layouts: 1.91 us -> 2.88 us
  transfers between devices with their start and end apart: 7 -> 4, of which waited for: 6 -> 4; matrix products, arithmetic and copies ran while one was open for 0% -> 0% of each run, Pallas kernels for 31% -> 13%
where the time goes in v2:
time: 81.8 us; the launch traced here: 81 us
  blocking collectives  34.8 us (43%)
  Pallas kernels  20 us (24%)
  waiting for transfers between devices  15.7 us (19%)
  local copies, waits for them, and re-layouts  5.08 us (6%)
  starting transfers between devices  4.59 us (6%)
    all_to_all x1, blocking collectives, reduced(): lax.all_to_all(part.reshape(count, rows // count, -1), axis, 0, 0, tiled=...  34.8 us
    all_to_all x1, waiting for transfers between devices, gathered(): lax.all_to_all(copies, axis, 0, 0, tiled=True).reshape(-1, piece.shape[1])  10.7 us
    pallas_call x1, Pallas kernels, grad_part(): pl.pallas_call(functools.partial(grad_kernel, shards, rows, most), out_sh...  10.7 us
    pallas_call x1, Pallas kernels, filter_part(): pl.pallas_call(functools.partial(filter_kernel, shards, rows, most, scale...  9.31 us
    ppermute x3, waiting for transfers between devices, shifted(): lax.ppermute(array, axis, [(i, (i + step) % count) for i in range(count)])  4.92 us
    all_to_all x1, starting transfers between devices, gathered(): lax.all_to_all(copies, axis, 0, 0, tiled=True).reshape(-1, piece.shape[1])  3.95 us
    unnamed x9, local copies, waits for them, and re-layouts  2.88 us
  transfers between devices with their start and end apart: 4, of which 4 were waited for; matrix products, arithmetic and copies ran while one was open for 0% of the time, Pallas kernels for 13%

profile of v2, /device:TPU:0, one launch (start us, length us, event | category | flops | bytes accessed | tf_op | source)
XLA Modules:
  0.0 81.0 jit_solution(17701836358222620810)
XLA Ops:
  0.6 0.6 collective-permute-start
  1.2 0.1 collective-permute-start.2
  1.3 2.4 %collective-permute-done.refs_1_.refs_3_ = bf16[1,128,4096]{2,1,0:T(8,128)(2,1)S(1)} collective-permute-done((bf16[1,128,4096]{2,1,0:T(8,128)(2,1)}, bf16[1,128,4096]{2,1,0:T(8,128)(2,1)S(1)}, u32[]{:S(2)}, u32[]{:S(2)}) %collective-permute-start) | collective-permute-done | bytes 1048608 | tf_op jit(solution)/shard_map/ppermute | solution.py:227
  3.7 0.0 copy-start.2
  3.7 1.5 %collective-permute-done.2.refs_1_ = bf16[1,128,4096]{2,1,0:T(8,128)(2,1)S(1)} collective-permute-done((bf16[1,128,4096]{2,1,0:T(8,128)(2,1)}, bf16[1,128,4096]{2,1,0:T(8,128)(2,1)S(1)}, u32[]{:S(2)}, u32[]{:S(2)}) %collective-permute-start.2) | collective-permute-done | bytes 1048608 | tf_op jit(solution)/shard_map/ppermute | solution.py:227
  5.2 0.0 copy-start.3
  5.2 0.0 copy-done.2
  5.2 1.0 %copy-done.3 = bf16[1,128,4096]{2,1,0:T(8,128)(2,1)} copy-done((bf16[1,128,4096]{2,1,0:T(8,128)(2,1)}, bf16[1,128,4096]{2,1,0:T(8,128)(2,1)S(1)}, u32[]{:S(2)}) %copy-start.3) | copy-done | bytes 1048600
  6.2 9.3 %shard_map.122 = f32[2048,128]{1,0:T(8,128)} custom-call(s32[1]{0:T(128)} %bitcast.me_ref, bf16[1,128,4096]{2,1,0:T(8,128)(2,1)} %refs_0_.3, bf16[1,128,4096]{2,1,0:T(8,128)(2,1)} %copy-done.3, bf16[1,128,4096]{2,1,0:T(8,128)(2,1)} %refs_2_.3, bf16[1,128,4096]{2,1,0:T(8,128)(2,1)} %copy-done.2, s32[1,256]{1,0:T(1,128)} %refs_4_.2, ...), custom_call_target="tpu_custom_call" | custom-call | flops 2550136832 | bytes 3145728 | tf_op jit(solution)/shard_map/pallas_call | solution.py:163
  15.5 34.8 %all_to_all.10 = f32[16,128,128]{2,1,0:T(8,128)S(1)} all-to-all(f32[16,128,128]{2,1,0:T(8,128)} %bitcast.6), channel_id=1, replica_groups=mesh['dp'=16,'ctx'=2] {'dp'}, dimensions={0} | all-to-all | bytes 2097152 | tf_op jit(solution)/shard_map/all_to_all | solution.py:233
  50.3 0.1 reduce_sum.9
  50.4 1.1 %broadcast_in_dim.14 = f32[16,128,128]{2,1,0:T(8,128)} broadcast(f32[128,128]{1,0:T(8,128)S(1)} %reduce_sum.9), dimensions={1,2} | broadcast | bytes 1114112 | tf_op jit(solution)/shard_map/broadcast_in_dim | solution.py:238
  51.4 3.9 %all-to-all-start.1 = ((f32[16,128,128]{2,1,0:T(8,128)}), f32[16,128,128]{2,1,0:T(8,128)S(1)}, u32[]{:S(2)}, u32[]{:S(2)}) async-start(f32[16,128,128]{2,1,0:T(8,128)} %broadcast_in_dim.14), calls=%async_computation.1 | async-start | bytes 2097152 | tf_op jit(solution)/shard_map/all_to_all | solution.py:239
  55.4 10.7 %shard_map.121 = (bf16[1,128,2048]{2,1,0:T(8,128)(2,1)}, bf16[1,128,2048]{2,1,0:T(8,128)(2,1)}) custom-call(s32[1]{0:T(128)} %bitcast.me_ref, bf16[1,128,4096]{2,1,0:T(8,128)(2,1)} %refs_2_.3, bf16[1,128,4096]{2,1,0:T(8,128)(2,1)} %copy-done.2, s32[1,256]{1,0:T(1,128)} %refs_4_.2, bf16[256,256]{1,0:T(8,128)(2,1)} %constant.23.clone.refs_3_.refs_4_.refs_5_, ...), custom_call_target="tpu_custom_call" | custom-call | flops 2952790016 | bytes 2621440 | tf_op jit(solution)/shard_map/pallas_call | solution.py:196
  66.1 0.0 collective-permute-start.1
  66.1 0.0 copy-start.1
  66.2 0.1 broadcast_in_dim.12
  66.3 0.9 %copy-done.1 = bf16[1,128,2048]{2,1,0:T(8,128)(2,1)S(1)} copy-done((bf16[1,128,2048]{2,1,0:T(8,128)(2,1)S(1)}, bf16[1,128,2048]{2,1,0:T(8,128)(2,1)}, u32[]{:S(2)}) %copy-start.1) | copy-done | bytes 524312
  67.2 1.0 %collective-permute-done.1 = bf16[1,128,2048]{2,1,0:T(8,128)(2,1)S(1)} collective-permute-done((bf16[1,128,2048]{2,1,0:T(8,128)(2,1)}, bf16[1,128,2048]{2,1,0:T(8,128)(2,1)S(1)}, u32[]{:S(2)}, u32[]{:S(2)}) %collective-permute-start.1) | collective-permute-done | bytes 524320 | tf_op jit(solution)/shard_map/ppermute | solution.py:227
  68.3 0.0 copy-start
  68.3 10.7 %all-to-all-done.1 = f32[16,128,128]{2,1,0:T(8,128)S(1)} async-done(((f32[16,128,128]{2,1,0:T(8,128)}), f32[16,128,128]{2,1,0:T(8,128)S(1)}, u32[]{:S(2)}, u32[]{:S(2)}) %all-to-all-start.1) | async-done | bytes 1048608 | tf_op jit(solution)/shard_map/all_to_all | solution.py:239
  79.1 0.9 %slice_reduce_fusion = f32[2048]{0:T(1024)} fusion(f32[2048,128]{1,0:T(8,128)S(1)} %bitcast.4), kind=kLoop, calls=%fused_computation | loop fusion | bytes 16384 | tf_op jit(solution)/shard_map/slice | solution.py:265
  80.0 1.0 %copy.16 = f32[2048,128]{1,0:T(8,128)} copy(f32[2048,128]{1,0:T(8,128)S(1)} %bitcast.5) | data formatting | bytes 2097152
  81.0 0.0 copy-done
  (2 shorter events, 0.1 us)
Async XLA Ops:
  0.6 3.1 %collective-permute-start = (bf16[1,128,4096]{2,1,0:T(8,128)(2,1)}, bf16[1,128,4096]{2,1,0:T(8,128)(2,1)S(1)}, u32[]{:S(2)}, u32[]{:S(2)}) collective-permute-start(bf16[1,128,4096]{2,1,0:T(8,128)(2,1)} %refs_2_.3), channel_id=1, source_target_pairs={{0,1},{1,0},{2,3},{3,2},{4,5},{5,4},{6,7},{7,6},{8,9},{9,8},{10,11... | collective-permute-start | bytes 3145736 | tf_op jit(solution)/shard_map/ppermute | solution.py:227
  1.2 4.0 %collective-permute-start.2 = (bf16[1,128,4096]{2,1,0:T(8,128)(2,1)}, bf16[1,128,4096]{2,1,0:T(8,128)(2,1)S(1)}, u32[]{:S(2)}, u32[]{:S(2)}) collective-permute-start(bf16[1,128,4096]{2,1,0:T(8,128)(2,1)} %refs_0_.3), channel_id=1, source_target_pairs={{0,1},{1,0},{2,3},{3,2},{4,5},{5,4},{6,7},{7,6},{8,9},{9,8},{10,11... | collective-permute-start | bytes 3145736 | tf_op jit(solution)/shard_map/ppermute | solution.py:227
  3.7 1.5 %copy-start.2 = (bf16[1,128,4096]{2,1,0:T(8,128)(2,1)}, bf16[1,128,4096]{2,1,0:T(8,128)(2,1)S(1)}, u32[]{:S(2)}) copy-start(bf16[1,128,4096]{2,1,0:T(8,128)(2,1)S(1)} %collective-permute-done.refs_1_.refs_3_) | copy-start | bytes 3145732
  5.2 1.0 %copy-start.3 = (bf16[1,128,4096]{2,1,0:T(8,128)(2,1)}, bf16[1,128,4096]{2,1,0:T(8,128)(2,1)S(1)}, u32[]{:S(2)}) copy-start(bf16[1,128,4096]{2,1,0:T(8,128)(2,1)S(1)} %collective-permute-done.2.refs_1_) | copy-start | bytes 3145732
  51.4 27.6 %all-to-all-start.1 = ((f32[16,128,128]{2,1,0:T(8,128)}), f32[16,128,128]{2,1,0:T(8,128)S(1)}, u32[]{:S(2)}, u32[]{:S(2)}) async-start(f32[16,128,128]{2,1,0:T(8,128)} %broadcast_in_dim.14), calls=%async_computation.1 | async-start | bytes 2097152 | tf_op jit(solution)/shard_map/all_to_all | solution.py:239
  66.1 2.1 %collective-permute-start.1 = (bf16[1,128,2048]{2,1,0:T(8,128)(2,1)}, bf16[1,128,2048]{2,1,0:T(8,128)(2,1)S(1)}, u32[]{:S(2)}, u32[]{:S(2)}) collective-permute-start(bf16[1,128,2048]{2,1,0:T(8,128)(2,1)} %get-tuple-element.6), channel_id=1, source_target_pairs={{0,1},{1,0},{2,3},{3,2},{4,5},{5,4},{6,7},{7,6},{8,9},{9,8},{10,11... | collective-permute-start | bytes 1572872 | tf_op jit(solution)/shard_map/ppermute | solution.py:227
  66.1 1.0 %copy-start.1 = (bf16[1,128,2048]{2,1,0:T(8,128)(2,1)S(1)}, bf16[1,128,2048]{2,1,0:T(8,128)(2,1)}, u32[]{:S(2)}) copy-start(bf16[1,128,2048]{2,1,0:T(8,128)(2,1)} %get-tuple-element.5) | copy-start | bytes 1572868
  68.3 12.7 %copy-start = (bf16[1,128,4096]{2,1,0:T(8,128)(2,1)}, bf16[1,128,4096]{2,1,0:T(8,128)(2,1)S(1)}, u32[]{:S(2)}) copy-start(bf16[1,128,4096]{2,1,0:T(8,128)(2,1)S(1)} %constant_dynamic-update-slice_fusion) | copy-start | bytes 3145732

commit v3 on v2

--- a/solution.py
+++ b/solution.py
@@ -13,6 +13,9 @@
 TILES = 2
 BLOCK = LANES * TILES
 DOCS = 4
+TOP = 12.0
+NOTE = STEP
+TINY = 1e-30
 
 
 def up(value, unit):
@@ -87,12 +90,20 @@
     return [lax.rem(me - k + count, count) for k in range(count)]
 
 
-def filter_kernel(shards, rows, most, scale, me_ref, *refs):
+def power(exponent):
+    return jnp.exp(exponent * math.log(2.0))
+
+
+def exponent_of(peak):
+    return jnp.ceil(jnp.log(jnp.maximum(peak, TINY)) * (1.0 / math.log(2.0)))
+
+
+def filter_kernel(shards, rows, most, scale, packed, me_ref, *refs):
     u_refs = refs[:shards]
     g_refs = refs[shards : 2 * shards]
     ids_ref, ahead_ref, back_ref, out_ref, info_ref, u_full, g_full = refs[2 * shards :]
     length = shards * rows
-    kernel = out_ref.shape[1]
+    kernel = LANES
 
     @pl.when(pl.program_id(0) == 0)
     def _():
@@ -111,9 +122,35 @@
         add_real, add_imag = against(g_wave, u_wave)
         real, imag = real + add_real, imag + add_imag
     taps = inverse(back_ref[:kernel, :], real, imag) * scale
+    if packed:
+        exponent = exponent_of(jnp.max(jnp.abs(taps), axis=0, keepdims=True))
+        taps = taps * power(TOP - exponent)
     for tile in range(TILES):
         at = tile * LANES
-        out_ref[at : at + LANES, :] = taps[:, at : at + LANES].T
+        if packed:
+            out_ref[tile, :kernel, :] = taps[:, at : at + LANES]
+            out_ref[tile, kernel:, :] = jnp.broadcast_to(exponent[:, at : at + LANES], (NOTE, LANES))
+        else:
+            out_ref[at : at + LANES, :] = taps[:, at : at + LANES].T
+
+
+def total_kernel(pieces_ref, out_ref):
+    kernel = pieces_ref.shape[1] - NOTE
+    total = jnp.zeros((kernel, LANES), jnp.float32)
+    for k in range(pieces_ref.shape[0]):
+        total = total + pieces_ref[k, :kernel, :] * power(pieces_ref[k, kernel : kernel + 1, :] - TOP)
+    peak = jnp.max(jnp.max(jnp.abs(total), axis=0, keepdims=True), axis=1, keepdims=True)
+    exponent = exponent_of(peak)
+    total = total * power(TOP - exponent)
+    out_ref[:LANES, :] = total.T
+    row = lax.broadcasted_iota(jnp.int32, (NOTE, LANES), 0)
+    out_ref[LANES:, :] = jnp.where(row == 0, exponent, total[:1, :])
+
+
+def total_part(pieces):
+    return pl.pallas_call(
+        total_kernel, out_shape=jax.ShapeDtypeStruct((LANES + NOTE, pieces.shape[1] - NOTE), jnp.float32)
+    )(pieces)
 
 
 def grad_kernel(shards, rows, most, me_ref, *refs):
@@ -151,23 +188,29 @@
             out_ref[0, :, lanes] = (total_ref[tile, pl.ds(at, rows), :] + skipped).astype(out_ref.dtype)
 
 
-def filter_part(me, u_list, g_list, ids, kernel, scale, width, first, count):
+def filter_part(me, u_list, g_list, ids, kernel, scale, width, packed):
     shards = len(u_list)
     rows = u_list[0].shape[1]
     length = shards * rows
     most = length // 2
     blocks = width // BLOCK
     ahead, back = tables(most, kernel)
-    data = pl.BlockSpec((1, rows, BLOCK), lambda c, me_ref: (0, 0, me_ref[0] * blocks + first + c))
+    data = pl.BlockSpec((1, rows, BLOCK), lambda c, me_ref: (0, 0, me_ref[0] * blocks + c))
     fixed = lambda array: pl.BlockSpec(array.shape, lambda c, me_ref: (0, 0))
+    if packed:
+        shape = (width // LANES, kernel + NOTE, LANES)
+        out_spec = pl.BlockSpec((TILES,) + shape[1:], lambda c, me_ref: (c, 0, 0))
+    else:
+        shape = (width, kernel)
+        out_spec = pl.BlockSpec((BLOCK, kernel), lambda c, me_ref: (c, 0))
     return pl.pallas_call(
-        functools.partial(filter_kernel, shards, rows, most, scale),
-        out_shape=jax.ShapeDtypeStruct((count * BLOCK, kernel), jnp.float32),
+        functools.partial(filter_kernel, shards, rows, most, scale, packed),
+        out_shape=jax.ShapeDtypeStruct(shape, jnp.float32),
         grid_spec=pltpu.PrefetchScalarGridSpec(
             num_scalar_prefetch=1,
-            grid=(count,),
+            grid=(blocks,),
             in_specs=[data] * (2 * shards) + [fixed(ids), fixed(ahead), fixed(back)],
-            out_specs=pl.BlockSpec((BLOCK, kernel), lambda c, me_ref: (c, 0)),
+            out_specs=out_spec,
             scratch_shapes=[
                 pltpu.SMEM((2 * DOCS,), jnp.int32),
                 pltpu.VMEM((TILES, length + most, LANES), jnp.float32),
@@ -175,14 +218,14 @@
             ],
         ),
         cost_estimate=pl.CostEstimate(
-            flops=2 * count * BLOCK * (2 * DOCS * ahead.size + kernel * back.shape[1]),
-            bytes_accessed=count * BLOCK * (4 * length + 4 * kernel),
+            flops=2 * width * (2 * DOCS * ahead.size + kernel * back.shape[1]),
+            bytes_accessed=width * (4 * length + 4 * kernel),
             transcendentals=0,
         ),
     )(me, *u_list, *g_list, ids, jnp.asarray(ahead), jnp.asarray(back))
 
 
-def grad_part(me, g_list, ids, taps, skip_gain, width, first, count):
+def grad_part(me, g_list, ids, taps, skip_gain, width):
     shards = len(g_list)
     rows = g_list[0].shape[1]
     kernel = taps.shape[1]
@@ -191,19 +234,19 @@
     blocks = width // BLOCK
     ahead, back = tables(most, kernel)
     head = np.concatenate([ahead[:, :kernel], ahead[:, most : most + kernel]], axis=1)
-    data = pl.BlockSpec((1, rows, BLOCK), lambda c, me_ref: (0, 0, me_ref[0] * blocks + first + c))
+    data = pl.BlockSpec((1, rows, BLOCK), lambda c, me_ref: (0, 0, me_ref[0] * blocks + c))
     fixed = lambda array: pl.BlockSpec(array.shape, lambda c, me_ref: (0, 0))
     return pl.pallas_call(
         functools.partial(grad_kernel, shards, rows, most),
-        out_shape=[jax.ShapeDtypeStruct((1, rows, count * BLOCK), jnp.bfloat16)] * shards,
+        out_shape=[jax.ShapeDtypeStruct((1, rows, width), jnp.bfloat16)] * shards,
         grid_spec=pltpu.PrefetchScalarGridSpec(
             num_scalar_prefetch=1,
-            grid=(count,),
+            grid=(blocks,),
             in_specs=[data] * shards
             + [fixed(ids), fixed(ahead), fixed(head), fixed(back)]
             + [
-                pl.BlockSpec((BLOCK, kernel), lambda c, me_ref: (me_ref[0] * blocks + first + c, 0)),
-                pl.BlockSpec((1, BLOCK), lambda c, me_ref: (0, me_ref[0] * blocks + first + c)),
+                pl.BlockSpec((BLOCK, kernel), lambda c, me_ref: (me_ref[0] * blocks + c, 0)),
+                pl.BlockSpec((1, BLOCK), lambda c, me_ref: (0, me_ref[0] * blocks + c)),
             ],
             out_specs=[pl.BlockSpec((1, rows, BLOCK), lambda c, me_ref: (0, 0, c))] * shards,
             scratch_shapes=[
@@ -213,30 +256,39 @@
             ],
         ),
         cost_estimate=pl.CostEstimate(
-            flops=2 * count * BLOCK * (DOCS * (ahead.size + back.size) + head.size),
-            bytes_accessed=count * BLOCK * (4 * length + 2 * kernel),
+            flops=2 * width * (DOCS * (ahead.size + back.size) + head.size),
+            bytes_accessed=width * (4 * length + 2 * kernel),
             transcendentals=0,
         ),
     )(me, *g_list, ids, jnp.asarray(ahead), jnp.asarray(head), jnp.asarray(back), taps, skip_gain.reshape(1, -1))
 
 
-CHUNKS = 1
-
-
 def shifted(array, axis, count, step):
     return lax.ppermute(array, axis, [(i, (i + step) % count) for i in range(count)])
 
 
-def reduced(part, axis, count):
-    rows = up(part.shape[0], count)
-    part = jnp.pad(part, ((0, rows - part.shape[0]), (0, 0)))
-    pieces = lax.all_to_all(part.reshape(count, rows // count, -1), axis, 0, 0, tiled=True)
-    return jnp.sum(pieces, axis=0)
-
-
-def gathered(piece, axis, count, rows):
-    copies = jnp.broadcast_to(piece[None], (count,) + piece.shape)
-    return lax.all_to_all(copies, axis, 0, 0, tiled=True).reshape(-1, piece.shape[1])[:rows]
+def exchanged(pieces, axis):
+    return lax.all_to_all(pieces, axis, 0, 0, tiled=True)
+
+
+def packed_sum(parts, axis, count):
+    pieces = exchanged(parts.astype(jnp.float16), axis).astype(jnp.float32)
+    piece = total_part(pieces).astype(jnp.float16)
+    pieces = exchanged(jnp.broadcast_to(piece[None], (count,) + piece.shape), axis)
+    pieces = pieces.astype(jnp.float32)
+    weight = power(pieces[:, LANES, :1] - TOP)
+    whole = pieces[:, :LANES, :] * weight[:, :, None]
+    skip = pieces[:, LANES + 1, :] * weight
+    return whole.reshape(count * LANES, -1), skip.reshape(-1)
+
+
+def plain_sum(parts, axis, count):
+    rows = up(parts.shape[0], count)
+    padded = jnp.pad(parts, ((0, rows - parts.shape[0]), (0, 0)))
+    piece = jnp.sum(exchanged(padded.reshape(count, rows // count, -1), axis), axis=0)
+    whole = exchanged(jnp.broadcast_to(piece[None], (count,) + piece.shape), axis)
+    whole = whole.reshape(rows, -1)[: parts.shape[0]]
+    return whole, whole[:, 0]
 
 
 def shards(inputs, cotangent, segment_ids, taps, skip_gain):
@@ -244,25 +296,20 @@
     groups = lax.axis_size("dp")
     me = lax.axis_index("ctx").astype(jnp.int32)[None]
     width = inputs.shape[2] // count
+    kernel = taps.shape[1]
     scale = 1.0 / (inputs.shape[0] * groups)
+    packed = width == groups * LANES and kernel == LANES
     u_list = [inputs] + [shifted(inputs, "ctx", count, k) for k in range(1, count)]
     g_list = [cotangent] + [shifted(cotangent, "ctx", count, k) for k in range(1, count)]
-    blocks = width // BLOCK
-    each = blocks // CHUNKS
-    kernel = taps.shape[1]
-    shares = []
-    for chunk in range(CHUNKS):
-        part = filter_part(me, u_list, g_list, segment_ids, kernel, scale, width, chunk * each, each)
-        shares.append(reduced(part, "dp", groups))
-    parts = grad_part(me, g_list, segment_ids, taps, skip_gain, width, 0, blocks)
-    whole = [gathered(share, "dp", groups, each * BLOCK) for share in shares]
-    taps_grad = jnp.concatenate(whole, axis=0)
+    parts = filter_part(me, u_list, g_list, segment_ids, kernel, scale, width, packed)
+    taps_grad, skip_grad = (packed_sum if packed else plain_sum)(parts, "dp", groups)
+    grads = grad_part(me, g_list, segment_ids, taps, skip_gain, width)
     input_grad = jnp.zeros(inputs.shape, jnp.bfloat16)
     for k in range(count):
-        got = parts[k] if k == 0 else shifted(parts[k], "ctx", count, -k)
-        owner = lax.rem(me[0] + k, count) if k else me[0]
+        got = grads[k] if k == 0 else shifted(grads[k], "ctx", count, -k)
+        owner = lax.rem(me[0] + k, count)
         input_grad = lax.dynamic_update_slice(input_grad, got, (0, 0, owner * width))
-    return input_grad, taps_grad, taps_grad[:, 0]
+    return input_grad, taps_grad, skip_grad
 
 
 def solution(mesh):

time: 81.8 us -> 68.2 us (0.83)
  blocking collectives: 34.8 us -> 25.1 us
  waiting for transfers between devices: 15.7 us -> 6.89 us
  other arithmetic: 0.06 us -> 5.34 us
  local copies, waits for them, and re-layouts: 5.08 us -> 2.9 us
  Pallas kernels: 20 us -> 22.1 us
    all_to_all x1, blocking collectives: 34.8 us -> 25.1 us  [exchanged(): return lax.all_to_all(pieces, axis, 0, 0, tiled=True)]
    all_to_all x1, waiting for transfers between devices: 10.7 us -> 1.88 us  [exchanged(): return lax.all_to_all(pieces, axis, 0, 0, tiled=True)]
    convert_element_type x0 -> x4, other arithmetic: none -> 3.35 us  [the longest x2 2.38 us: packed_sum(): pieces = exchanged(parts.astype(jnp.float16), axis).astype(jnp.float32)]
    pallas_call x0 -> x1, Pallas kernels: none -> 2.16 us  [total_part(): pl.pallas_call(total_kernel, out_shape=jax.ShapeDtypeStruct((LANES + NOTE...]
    mul x0 -> x2, other arithmetic: none -> 1.78 us  [the longest x1 1.11 us: packed_sum(): whole = pieces[:, :LANES, :] * weight[:, :, None]]
    unnamed x9 -> x8, local copies, waits for them, and re-layouts: 2.88 us -> 1.82 us
    slice x1, local copies, waits for them, and re-layouts: 0.94 us -> 0.01 us  [packed_sum(): skip = pieces[:, LANES + 1, :] * weight]
  transfers between devices with their start and end apart: 4 -> 4, of which waited for: 4 -> 4; matrix products, arithmetic and copies ran while one was open for 0% -> 0% of each run, Pallas kernels for 13% -> 16%
where the time goes in v3:
time: 68.2 us; the launch traced here: 67.4 us
  blocking collectives  25.1 us (37%)
  Pallas kernels  22.1 us (32%)
  waiting for transfers between devices  6.89 us (10%)
  other arithmetic  5.34 us (8%)
  starting transfers between devices  4.29 us (6%)
  local copies, waits for them, and re-layouts  2.9 us (4%)
  between operations  0.72 us (1%)
    all_to_all x1, blocking collectives, exchanged(): return lax.all_to_all(pieces, axis, 0, 0, tiled=True)  25.1 us
    pallas_call x1, Pallas kernels, grad_part(): pl.pallas_call(functools.partial(grad_kernel, shards, rows, most), out_sh...  10.7 us
    pallas_call x1, Pallas kernels, filter_part(): pl.pallas_call(functools.partial(filter_kernel, shards, rows, most, scale...  9.18 us
    ppermute x3, waiting for transfers between devices, shifted(): lax.ppermute(array, axis, [(i, (i + step) % count) for i in range(count)])  5.01 us
    all_to_all x1, starting transfers between devices, exchanged(): return lax.all_to_all(pieces, axis, 0, 0, tiled=True)  3.58 us
    convert_element_type x2, other arithmetic, packed_sum(): pieces = exchanged(parts.astype(jnp.float16), axis).astype(jnp.float32)  2.38 us
    pallas_call x1, Pallas kernels, total_part(): pl.pallas_call(total_kernel, out_shape=jax.ShapeDtypeStruct((LANES + NOTE...  2.16 us
    all_to_all x1, waiting for transfers between devices, exchanged(): return lax.all_to_all(pieces, axis, 0, 0, tiled=True)  1.88 us
  transfers between devices with their start and end apart: 4, of which 4 were waited for; matrix products, arithmetic and copies ran while one was open for 0% of the time, Pallas kernels for 16%

profile of v3, /device:TPU:0, one launch (start us, length us, event | category | flops | bytes accessed | tf_op | source)
XLA Modules:
  0.0 67.4 jit_solution(2648935902003006955)
XLA Ops:
  0.6 0.6 collective-permute-start
  1.2 0.1 collective-permute-start.2
  1.3 2.4 %collective-permute-done.refs_1_.refs_3_ = bf16[1,128,4096]{2,1,0:T(8,128)(2,1)S(1)} collective-permute-done((bf16[1,128,4096]{2,1,0:T(8,128)(2,1)}, bf16[1,128,4096]{2,1,0:T(8,128)(2,1)S(1)}, u32[]{:S(2)}, u32[]{:S(2)}) %collective-permute-start) | collective-permute-done | bytes 1048608 | tf_op jit(solution)/shard_map/ppermute | solution.py:267
  3.7 0.0 copy-start.2
  3.7 1.5 %collective-permute-done.2.refs_1_ = bf16[1,128,4096]{2,1,0:T(8,128)(2,1)S(1)} collective-permute-done((bf16[1,128,4096]{2,1,0:T(8,128)(2,1)}, bf16[1,128,4096]{2,1,0:T(8,128)(2,1)S(1)}, u32[]{:S(2)}, u32[]{:S(2)}) %collective-permute-start.2) | collective-permute-done | bytes 1048608 | tf_op jit(solution)/shard_map/ppermute | solution.py:267
  5.2 0.0 copy-start.3
  5.2 0.0 copy-done.2
  5.2 1.0 %copy-done.3 = bf16[1,128,4096]{2,1,0:T(8,128)(2,1)} copy-done((bf16[1,128,4096]{2,1,0:T(8,128)(2,1)}, bf16[1,128,4096]{2,1,0:T(8,128)(2,1)S(1)}, u32[]{:S(2)}) %copy-start.3) | copy-done | bytes 1048600
  6.2 9.2 %shard_map.122 = f32[16,136,128]{2,1,0:T(8,128)} custom-call(s32[1]{0:T(128)} %bitcast.me_ref, bf16[1,128,4096]{2,1,0:T(8,128)(2,1)} %refs_0_.3, bf16[1,128,4096]{2,1,0:T(8,128)(2,1)} %copy-done.3, bf16[1,128,4096]{2,1,0:T(8,128)(2,1)} %refs_2_.3, bf16[1,128,4096]{2,1,0:T(8,128)(2,1)} %copy-done.2, s32[1,256]{1,0:T(1,128)} %refs_4_.2, ...), custom_call_target="tpu_custom_call" | custom-call | flops 2550136832 | bytes 3145728 | tf_op jit(solution)/shard_map/pallas_call | solution.py:206
  15.3 1.3 %convert_element_type.12 = f16[16,136,128]{2,1,0:T(8,128)(2,1)S(1)} convert(f32[16,136,128]{2,1,0:T(8,128)} %shard_map.122) | non-fusion elementwise | flops 278528 | bytes 1671168 | tf_op jit(solution)/shard_map/convert_element_type | solution.py:275
  16.7 25.1 %all_to_all.10 = f16[16,136,128]{2,1,0:T(8,128)(2,1)S(1)} all-to-all(f16[16,136,128]{2,1,0:T(8,128)(2,1)S(1)} %convert_element_type.12), channel_id=1, replica_groups=mesh['dp'=16,'ctx'=2] {'dp'}, dimensions={0} | all-to-all | bytes 1114112 | tf_op jit(solution)/shard_map/all_to_all | solution.py:271
  41.8 1.1 %convert_element_type.13.pieces_ref = f32[16,136,128]{2,1,0:T(8,128)} convert(f16[16,136,128]{2,1,0:T(8,128)(2,1)S(1)} %all_to_all.10) | non-fusion elementwise | flops 278528 | bytes 1671168 | tf_op jit(solution)/shard_map/convert_element_type | solution.py:275
  42.9 2.2 %shard_map.123 = f32[136,128]{1,0:T(8,128)} custom-call(f32[16,136,128]{2,1,0:T(8,128)} %convert_element_type.13.pieces_ref), custom_call_target="tpu_custom_call" | custom-call | tf_op jit(solution)/shard_map/pallas_call | solution.py:151
  45.0 0.9 %convert_element_type.14 = f16[136,128]{1,0:T(8,128)(2,1)S(1)} convert(f32[136,128]{1,0:T(8,128)} %shard_map.123) | non-fusion elementwise | flops 17408 | bytes 104448 | tf_op jit(solution)/shard_map/convert_element_type | solution.py:276
  45.9 0.9 %broadcast_in_dim.15 = f16[16,136,128]{2,1,0:T(8,128)(2,1)} broadcast(f16[136,128]{1,0:T(8,128)(2,1)S(1)} %convert_element_type.14), dimensions={1,2} | broadcast | bytes 591872 | tf_op jit(solution)/shard_map/broadcast_in_dim | solution.py:277
  46.8 3.6 %all-to-all-start.1 = ((f16[16,136,128]{2,1,0:T(8,128)(2,1)}), f16[16,136,128]{2,1,0:T(8,128)(2,1)S(1)}, u32[]{:S(2)}, u32[]{:S(2)}) async-start(f16[16,136,128]{2,1,0:T(8,128)(2,1)} %broadcast_in_dim.15), calls=%async_computation.1 | async-start | bytes 1114112 | tf_op jit(solution)/shard_map/all_to_all | solution.py:271
  50.4 10.7 %shard_map.121 = (bf16[1,128,2048]{2,1,0:T(8,128)(2,1)}, bf16[1,128,2048]{2,1,0:T(8,128)(2,1)}) custom-call(s32[1]{0:T(128)} %bitcast.me_ref, bf16[1,128,4096]{2,1,0:T(8,128)(2,1)} %refs_2_.3, bf16[1,128,4096]{2,1,0:T(8,128)(2,1)} %copy-done.2, s32[1,256]{1,0:T(1,128)} %refs_4_.2, bf16[256,256]{1,0:T(8,128)(2,1)} %constant.28.clone.refs_3_.refs_4_.refs_5_, ...), custom_call_target="tpu_custom_call" | custom-call | flops 2952790016 | bytes 2621440 | tf_op jit(solution)/shard_map/pallas_call | solution.py:239
  61.1 0.0 copy-start.1
  61.1 0.1 collective-permute-start.1
  61.2 0.1 broadcast_in_dim.6
  61.3 0.8 %copy-done.1 = bf16[1,128,2048]{2,1,0:T(8,128)(2,1)S(1)} copy-done((bf16[1,128,2048]{2,1,0:T(8,128)(2,1)S(1)}, bf16[1,128,2048]{2,1,0:T(8,128)(2,1)}, u32[]{:S(2)}) %copy-start.1) | copy-done | bytes 524312
  62.2 1.1 %collective-permute-done.1 = bf16[1,128,2048]{2,1,0:T(8,128)(2,1)S(1)} collective-permute-done((bf16[1,128,2048]{2,1,0:T(8,128)(2,1)}, bf16[1,128,2048]{2,1,0:T(8,128)(2,1)S(1)}, u32[]{:S(2)}, u32[]{:S(2)}) %collective-permute-start.1) | collective-permute-done | bytes 524320 | tf_op jit(solution)/shard_map/ppermute | solution.py:267
  63.4 0.0 copy-start
  63.4 1.9 %all-to-all-done.1 = f16[16,136,128]{2,1,0:T(8,128)(2,1)S(1)} async-done(((f16[16,136,128]{2,1,0:T(8,128)(2,1)}), f16[16,136,128]{2,1,0:T(8,128)(2,1)S(1)}, u32[]{:S(2)}, u32[]{:S(2)}) %all-to-all-start.1) | async-done | bytes 557088 | tf_op jit(solution)/shard_map/all_to_all | solution.py:271
  65.3 0.1 convert_element_type.15
  65.3 0.2 fusion.2
  65.6 1.1 %slice_multiply_fusion = f32[16,128,128]{2,1,0:T(8,128)} fusion(f32[16,136,128]{2,1,0:T(8,128)S(1)} %convert_element_type.15, f32[16]{0:T(128)S(1)} %fusion.2), kind=kLoop, calls=%fused_computation | loop fusion | flops 262144 | bytes 2097216 | tf_op jit(solution)/shard_map/mul | solution.py:280
  66.7 0.0 copy-done
  66.7 0.7 bitcast_multiply_fusion
  (3 shorter events, 0.1 us)
Async XLA Ops:
  0.6 3.1 %collective-permute-start = (bf16[1,128,4096]{2,1,0:T(8,128)(2,1)}, bf16[1,128,4096]{2,1,0:T(8,128)(2,1)S(1)}, u32[]{:S(2)}, u32[]{:S(2)}) collective-permute-start(bf16[1,128,4096]{2,1,0:T(8,128)(2,1)} %refs_2_.3), channel_id=1, source_target_pairs={{0,1},{1,0},{2,3},{3,2},{4,5},{5,4},{6,7},{7,6},{8,9},{9,8},{10,11... | collective-permute-start | bytes 3145736 | tf_op jit(solution)/shard_map/ppermute | solution.py:267
  1.2 4.0 %collective-permute-start.2 = (bf16[1,128,4096]{2,1,0:T(8,128)(2,1)}, bf16[1,128,4096]{2,1,0:T(8,128)(2,1)S(1)}, u32[]{:S(2)}, u32[]{:S(2)}) collective-permute-start(bf16[1,128,4096]{2,1,0:T(8,128)(2,1)} %refs_0_.3), channel_id=1, source_target_pairs={{0,1},{1,0},{2,3},{3,2},{4,5},{5,4},{6,7},{7,6},{8,9},{9,8},{10,11... | collective-permute-start | bytes 3145736 | tf_op jit(solution)/shard_map/ppermute | solution.py:267
  3.7 1.5 %copy-start.2 = (bf16[1,128,4096]{2,1,0:T(8,128)(2,1)}, bf16[1,128,4096]{2,1,0:T(8,128)(2,1)S(1)}, u32[]{:S(2)}) copy-start(bf16[1,128,4096]{2,1,0:T(8,128)(2,1)S(1)} %collective-permute-done.refs_1_.refs_3_) | copy-start | bytes 3145732
  5.2 1.0 %copy-start.3 = (bf16[1,128,4096]{2,1,0:T(8,128)(2,1)}, bf16[1,128,4096]{2,1,0:T(8,128)(2,1)S(1)}, u32[]{:S(2)}) copy-start(bf16[1,128,4096]{2,1,0:T(8,128)(2,1)S(1)} %collective-permute-done.2.refs_1_) | copy-start | bytes 3145732
  46.8 18.5 %all-to-all-start.1 = ((f16[16,136,128]{2,1,0:T(8,128)(2,1)}), f16[16,136,128]{2,1,0:T(8,128)(2,1)S(1)}, u32[]{:S(2)}, u32[]{:S(2)}) async-start(f16[16,136,128]{2,1,0:T(8,128)(2,1)} %broadcast_in_dim.15), calls=%async_computation.1 | async-start | bytes 1114112 | tf_op jit(solution)/shard_map/all_to_all | solution.py:271
  61.1 1.0 %copy-start.1 = (bf16[1,128,2048]{2,1,0:T(8,128)(2,1)S(1)}, bf16[1,128,2048]{2,1,0:T(8,128)(2,1)}, u32[]{:S(2)}) copy-start(bf16[1,128,2048]{2,1,0:T(8,128)(2,1)} %get-tuple-element.5) | copy-start | bytes 1572868
  61.1 2.2 %collective-permute-start.1 = (bf16[1,128,2048]{2,1,0:T(8,128)(2,1)}, bf16[1,128,2048]{2,1,0:T(8,128)(2,1)S(1)}, u32[]{:S(2)}, u32[]{:S(2)}) collective-permute-start(bf16[1,128,2048]{2,1,0:T(8,128)(2,1)} %get-tuple-element.6), channel_id=1, source_target_pairs={{0,1},{1,0},{2,3},{3,2},{4,5},{5,4},{6,7},{7,6},{8,9},{9,8},{10,11... | collective-permute-start | bytes 1572872 | tf_op jit(solution)/shard_map/ppermute | solution.py:267
  63.4 3.3 %copy-start = (bf16[1,128,4096]{2,1,0:T(8,128)(2,1)}, bf16[1,128,4096]{2,1,0:T(8,128)(2,1)S(1)}, u32[]{:S(2)}) copy-start(bf16[1,128,4096]{2,1,0:T(8,128)(2,1)S(1)} %constant_dynamic-update-slice_fusion) | copy-start | bytes 3145732

commit v4 on v3

v4 whole, which is shorter than its diff:
```python
import functools
import math
import jax
import jax.numpy as jnp
import numpy as np
from jax import lax
from jax.experimental import pallas as pl
from jax.experimental.pallas import tpu as pltpu
from jax.sharding import PartitionSpec as P

LANES = 128
STEP = 8
TILES = 2
SUBS = 2
BLOCK = LANES * TILES
DOCS = 4
TOP = 12.0
NOTE = STEP
TINY = 1e-30


def up(value, unit):
    return -(-value // unit) * unit


def halves(table):
    high = np.asarray(table, np.float32).astype(jnp.bfloat16)
    low = (np.asarray(table, np.float64) - high.astype(np.float64)).astype(np.float32).astype(jnp.bfloat16)
    return high, low


def tables(most, kernel):
    period = most + kernel
    waves = period // 2
    angle = np.pi * np.outer(2 * np.arange(waves) + 1, np.arange(most)) / period
    pair = np.stack([np.cos(angle).reshape(-1, STEP, most), -np.sin(angle).reshape(-1, STEP, most)], axis=1)
    pair = pair.reshape(period, most)
    ahead = np.concatenate(halves(pair), axis=1)
    back = halves(pair.T / waves)
    back = np.concatenate([back[0], back[0], back[1]], axis=1)
    return ahead, back


def spectrum(table, value):
    return jnp.dot(table, jnp.concatenate([value, value], axis=0), preferred_element_type=jnp.float32)


def against(left, right):
    product = []
    for at in range(0, left.shape[0], 2 * STEP):
        lr, li = left[at : at + STEP], left[at + STEP : at + 2 * STEP]
        rr, ri = right[at : at + STEP], right[at + STEP : at + 2 * STEP]
        product += [lr * rr + li * ri, li * rr - lr * ri]
    return product


def inverse(table, product):
    high, low = [], []
    for at in range(0, len(product), 2):
        value = jnp.concatenate(product[at : at + 2], axis=0)
        high.append(value.astype(jnp.bfloat16))
        low.append((value - high[-1].astype(jnp.float32)).astype(jnp.bfloat16))
    return jnp.dot(table, jnp.concatenate(high + low + high, axis=0), preferred_element_type=jnp.float32)


def documents(ids_ref, info_ref):
    ids = ids_ref[...]
    begin = jnp.int32(0)
    for doc in range(DOCS):
        count = jnp.sum(jnp.where(ids == doc, 1.0, 0.0)).astype(jnp.int32)
        info_ref[doc] = begin
        info_ref[DOCS + doc] = count
        begin = begin + count


def widen(refs, shards, rows, full_ref, sub, base):
    for k, (ref, shard) in enumerate(zip(refs, shards)):
        at = pl.multiple_of(shard * rows, STEP)
        for tile in range(TILES):
            first = sub * BLOCK + tile * LANES
            if k:
                first = pl.multiple_of(base + first, LANES)
            block = ref[0, :, pl.ds(first, LANES)]
            full_ref[tile, pl.ds(at, rows), :] = block.astype(jnp.float32)


def window(full_ref, begin, most, count=None):
    tiles = []
    for tile in range(TILES):
        column = [full_ref[tile, pl.ds(begin + i, STEP), :] for i in range(0, most, STEP)]
        tiles.append(jnp.concatenate(column, axis=0))
    value = jnp.concatenate(tiles, axis=1)
    if count is not None:
        value = jnp.where(lax.broadcasted_iota(jnp.int32, value.shape, 0) < count, value, 0.0)
    return value.astype(jnp.bfloat16)


def sources(me, count):
    return [lax.rem(me - k + count, count) for k in range(count)]


def power(exponent):
    return jnp.exp(exponent * math.log(2.0))


def exponent_of(peak):
    return jnp.ceil(jnp.log(jnp.maximum(peak, TINY)) * (1.0 / math.log(2.0)))


def filter_kernel(shards, rows, most, scale, packed, me_ref, *refs):
    u_refs = refs[:shards]
    g_refs = refs[shards : 2 * shards]
    ids_ref, ahead_ref, back_ref, out_ref, info_ref, u_all, g_all = refs[2 * shards :]
    length = shards * rows
    kernel = LANES

    @pl.when(pl.program_id(0) == 0)
    def _():
        documents(ids_ref, info_ref)
        u_all[:, :, length:, :] = jnp.zeros(u_all.shape[:2] + (most, LANES), jnp.float32)

    order = sources(me_ref[0], shards)
    wide = SUBS * BLOCK
    base = (me_ref[0] * pl.num_programs(0) + pl.program_id(0)) * wide
    ahead = ahead_ref[...]
    for sub in range(u_all.shape[0]):
        u_full, g_full = u_all.at[sub], g_all.at[sub]
        widen(u_refs, order, rows, u_full, sub, base)
        widen(g_refs, order, rows, g_full, sub, base)
        product = None
        for doc in range(DOCS):
            begin = info_ref[doc]
            g_wave = spectrum(ahead, window(g_full, begin, most, info_ref[DOCS + doc]))
            u_wave = spectrum(ahead, window(u_full, begin, most))
            more = against(g_wave, u_wave)
            product = more if product is None else [old + new for old, new in zip(product, more)]
        taps = inverse(back_ref[:kernel, :], product) * scale
        if packed:
            exponent = exponent_of(jnp.max(jnp.abs(taps), axis=0, keepdims=True))
            taps = taps * power(TOP - exponent)
        for tile in range(TILES):
            at = tile * LANES
            if packed:
                slot = (pl.program_id(0) * SUBS + sub) * TILES + tile
                out_ref[slot, :kernel, :] = taps[:, at : at + LANES]
                out_ref[slot, kernel:, :] = jnp.broadcast_to(exponent[:, at : at + LANES], (NOTE, LANES))
            else:
                out_ref[sub * BLOCK + at : sub * BLOCK + at + LANES, :] = taps[:, at : at + LANES].T


def grad_kernel(shards, rows, most, me_ref, *refs):
    g_refs = refs[:shards]
    ids_ref, ahead_ref, head_ref, back_ref, taps_ref, skip_ref = refs[shards : shards + 6]
    out_refs = refs[shards + 6 : 2 * shards + 6]
    info_ref, g_all, total_all = refs[2 * shards + 6 :]

    @pl.when(pl.program_id(0) == 0)
    def _():
        documents(ids_ref, info_ref)

    order = sources(me_ref[0], shards)
    wide = SUBS * BLOCK
    base = (me_ref[0] * pl.num_programs(0) + pl.program_id(0)) * wide
    ahead = ahead_ref[...]
    for sub in range(g_all.shape[0]):
        g_full, total_ref = g_all.at[sub], total_all.at[sub]
        widen(g_refs, order, rows, g_full, sub, base)
        taps = taps_ref[sub * BLOCK : (sub + 1) * BLOCK, :]
        h_wave = lax.dot_general(
            head_ref[...],
            jnp.concatenate([taps, taps], axis=1),
            (((1,), (1,)), ((), ())),
            preferred_element_type=jnp.float32,
        )
        for doc in range(DOCS):
            begin = info_ref[doc]
            g_wave = spectrum(ahead, window(g_full, begin, most, info_ref[DOCS + doc]))
            total = inverse(back_ref[...], against(g_wave, h_wave))
            for tile in range(TILES):
                for i in range(0, most, STEP):
                    total_ref[tile, pl.ds(begin + i, STEP), :] = total[i : i + STEP, tile * LANES : (tile + 1) * LANES]
        for out_ref, shard in zip(out_refs, order):
            at = pl.multiple_of(shard * rows, STEP)
            for tile in range(TILES):
                first = sub * BLOCK + tile * LANES
                lanes = slice(first, first + LANES)
                skipped = g_full[tile, pl.ds(at, rows), :] * skip_ref[:, lanes]
                out_ref[0, :, lanes] = (total_ref[tile, pl.ds(at, rows), :] + skipped).astype(out_ref.dtype)


def filter_part(me, u_list, g_list, ids, kernel, scale, width, packed):
    shards = len(u_list)
    rows = u_list[0].shape[1]
    length = shards * rows
    most = length // 2
    wide = SUBS * BLOCK
    blocks = width // wide
    ahead, back = tables(most, kernel)
    data = pl.BlockSpec((1, rows, wide), lambda c, me_ref: (0, 0, me_ref[0] * blocks + c))
    got = pl.BlockSpec(memory_space=pltpu.VMEM)
    fixed = lambda array: pl.BlockSpec(array.shape, lambda c, me_ref: (0, 0))
    if packed:
        shape = (width // LANES, kernel + NOTE, LANES)
        out_spec = pl.BlockSpec(memory_space=pltpu.VMEM)
        out_type = pltpu.VMEM(shape, jnp.float32)
    else:
        shape = (width, kernel)
        out_type = jax.ShapeDtypeStruct(shape, jnp.float32)
        out_spec = pl.BlockSpec((wide, kernel), lambda c, me_ref: (c, 0))
    return pl.pallas_call(
        functools.partial(filter_kernel, shards, rows, most, scale, packed),
        out_shape=out_type,
        grid_spec=pltpu.PrefetchScalarGridSpec(
            num_scalar_prefetch=1,
            grid=(blocks,),
            in_specs=([data] + [got] * (shards - 1)) * 2 + [fixed(ids), fixed(ahead), fixed(back)],
            out_specs=out_spec,
            scratch_shapes=[
                pltpu.SMEM((2 * DOCS,), jnp.int32),
                pltpu.VMEM((SUBS, TILES, length + most, LANES), jnp.float32),
                pltpu.VMEM((SUBS, TILES, length + most, LANES), jnp.float32),
            ],
        ),
        cost_estimate=pl.CostEstimate(
            flops=2 * width * (2 * DOCS * ahead.size + kernel * back.shape[1]),
            bytes_accessed=width * (4 * length + 4 * kernel),
            transcendentals=0,
        ),
    )(me, *u_list, *g_list, ids, jnp.asarray(ahead), jnp.asarray(back))


def grad_part(me, g_list, ids, taps, skip_gain, width):
    shards = len(g_list)
    rows = g_list[0].shape[1]
    kernel = taps.shape[1]
    length = shards * rows
    most = length // 2
    wide = SUBS * BLOCK
    blocks = width // wide
    ahead, back = tables(most, kernel)
    head = np.concatenate([ahead[:, :kernel], ahead[:, most : most + kernel]], axis=1)
    data = pl.BlockSpec((1, rows, wide), lambda c, me_ref: (0, 0, me_ref[0] * blocks + c))
    got = pl.BlockSpec(memory_space=pltpu.VMEM)
    fixed = lambda array: pl.BlockSpec(array.shape, lambda c, me_ref: (0, 0))
    return pl.pallas_call(
        functools.partial(grad_kernel, shards, rows, most),
        out_shape=[jax.ShapeDtypeStruct((1, rows, width), jnp.bfloat16)] * shards,
        grid_spec=pltpu.PrefetchScalarGridSpec(
            num_scalar_prefetch=1,
            grid=(blocks,),
            in_specs=[data] + [got] * (shards - 1)
            + [fixed(ids), fixed(ahead), fixed(head), fixed(back)]
            + [
                pl.BlockSpec((wide, kernel), lambda c, me_ref: (me_ref[0] * blocks + c, 0)),
                pl.BlockSpec((1, wide), lambda c, me_ref: (0, me_ref[0] * blocks + c)),
            ],
            out_specs=[pl.BlockSpec((1, rows, wide), lambda c, me_ref: (0, 0, c))] * shards,
            scratch_shapes=[
                pltpu.SMEM((2 * DOCS,), jnp.int32),
                pltpu.VMEM((SUBS, TILES, length + most, LANES), jnp.float32),
                pltpu.VMEM((SUBS, TILES, length + most, LANES), jnp.float32),
            ],
        ),
        cost_estimate=pl.CostEstimate(
            flops=2 * width * (DOCS * (ahead.size + back.size) + head.size),
            bytes_accessed=width * (4 * length + 2 * kernel),
            transcendentals=0,
        ),
    )(me, *g_list, ids, jnp.asarray(ahead), jnp.asarray(head), jnp.asarray(back), taps, skip_gain.reshape(1, -1))


def shifted(array, axis, count, step):
    return lax.ppermute(array, axis, [(i, (i + step) % count) for i in range(count)])


def exchanged(pieces, axis):
    return lax.all_to_all(pieces, axis, 0, 0, tiled=True)


def packed_sum(pieces):
    pieces = pieces.astype(jnp.float32)
    weights = power(pieces[:, LANES : LANES + 1, :] - TOP)
    total = jnp.sum(pieces[:, :LANES, :] * weights, axis=0)
    turned = total.T
    exponents = exponent_of(jnp.max(jnp.abs(turned), axis=0, keepdims=True))
    skip = total[:1, :] * power(TOP - exponents[:, :1])
    note = jnp.where(jnp.arange(NOTE)[:, None] == 0, exponents, skip)
    return jnp.concatenate([turned * power(TOP - exponents), note], axis=0)


def packed_whole(pieces):
    pieces = pieces.astype(jnp.float32)
    weights = power(pieces[:, LANES : LANES + 1, :] - TOP)
    whole = pieces[:, :LANES, :] * weights
    skip = pieces[:, LANES + 1, :] * weights[:, 0, :1]
    return whole.reshape(-1, whole.shape[2]), skip.reshape(-1)


def plain_sum(parts, axis, count):
    rows = up(parts.shape[0], count)
    padded = jnp.pad(parts, ((0, rows - parts.shape[0]), (0, 0)))
    piece = jnp.sum(exchanged(padded.reshape(count, rows // count, -1), axis), axis=0)
    whole = exchanged(jnp.broadcast_to(piece[None], (count,) + piece.shape), axis)
    whole = whole.reshape(rows, -1)[: parts.shape[0]]
    return whole, whole[:, 0]


def shards(inputs, cotangent, segment_ids, taps, skip_gain):
    count = lax.axis_size("ctx")
    groups = lax.axis_size("dp")
    me = lax.axis_index("ctx").astype(jnp.int32)[None]
    width = inputs.shape[2] // count
    kernel = taps.shape[1]
    scale = 1.0 / (inputs.shape[0] * groups)
    packed = width == groups * LANES and kernel == LANES
    held = lambda array: pltpu.with_memory_space_constraint(array, pltpu.VMEM) if packed else array
    u_list = [inputs] + [held(shifted(inputs, "ctx", count, k)) for k in range(1, count)]
    g_list = [cotangent] + [held(shifted(cotangent, "ctx", count, k)) for k in range(1, count)]
    parts = filter_part(me, u_list, g_list, segment_ids, kernel, scale, width, packed)
    if packed:
        pieces = exchanged(parts.astype(jnp.float16), "dp")
    grads = grad_part(me, g_list, segment_ids, taps, skip_gain, width)
    if packed:
        share = packed_sum(pieces)
        share = jnp.broadcast_to(share[None], (groups,) + share.shape).astype(jnp.float16)
        taps_grad, skip_grad = packed_whole(exchanged(share, "dp"))
    else:
        taps_grad, skip_grad = plain_sum(parts, "dp", groups)
    input_grad = jnp.zeros(inputs.shape, jnp.bfloat16)
    for k in range(count):
        got = grads[k] if k == 0 else shifted(grads[k], "ctx", count, -k)
        owner = lax.rem(me[0] + k, count)
        input_grad = lax.dynamic_update_slice(input_grad, got, (0, 0, owner * width))
    return input_grad, taps_grad, skip_grad


def solution(mesh):
    return jax.shard_map(
        shards,
        mesh=mesh,
        in_specs=(P("dp", "ctx", None), P("dp", "ctx", None), P("dp", None), P(), P()),
        out_specs=(P("dp", "ctx", None), P("ctx", None), P("ctx")),
        check_vma=False,
    )
```

time: 68.2 us -> 59.8 us (0.88)
  blocking collectives: 25.1 us -> 0 us
  waiting for transfers between devices: 6.89 us -> 24.8 us
  starting transfers between devices: 4.29 us -> 13 us
  Pallas kernels: 22.1 us -> 15.3 us
  other arithmetic: 5.34 us -> 3.23 us
    all_to_all x1 -> x0, blocking collectives: 25.1 us -> none  [exchanged(): return lax.all_to_all(pieces, axis, 0, 0, tiled=True)]
    all_to_all x1 -> x2, waiting for transfers between devices: 1.88 us -> 19.8 us  [exchanged(): return lax.all_to_all(pieces, axis, 0, 0, tiled=True)]
    all_to_all x1 -> x2, starting transfers between devices: 3.58 us -> 12.3 us  [exchanged(): return lax.all_to_all(pieces, axis, 0, 0, tiled=True)]
    pallas_call x1, Pallas kernels: 9.18 us -> 6.44 us  [filter_part(): pl.pallas_call(functools.partial(filter_kernel, shards, rows, most, scale...]
    convert_element_type x3 -> x2, other arithmetic: 3.27 us -> 0.95 us  [the longest x1 0.88 us: shards(): pieces = exchanged(parts.astype(jnp.float16), 'dp')]
    pallas_call x1 -> x0, Pallas kernels: 2.16 us -> none  [total_part(): pl.pallas_call(total_kernel, out_shape=jax.ShapeDtypeStruct((LANES + NOTE...]
    pallas_call x1, Pallas kernels: 10.7 us -> 8.89 us  [grad_part(): pl.pallas_call(functools.partial(grad_kernel, shards, rows, most), out_sh...]
    unnamed x8 -> x4, local copies, waits for them, and re-layouts: 1.82 us -> 0.87 us
  transfers between devices with their start and end apart: 4 -> 5, of which waited for: 4 -> 5; matrix products, arithmetic and copies ran while one was open for 0% -> 0% of each run, Pallas kernels for 16% -> 15%
where the time goes in v4:
time: 59.8 us; the launch traced here: 59.4 us
  waiting for transfers between devices  24.8 us (41%)
  Pallas kernels  15.3 us (26%)
  starting transfers between devices  13 us (22%)
  other arithmetic  3.23 us (5%)
  local copies, waits for them, and re-layouts  2.27 us (4%)
  between operations  0.89 us (1%)
    all_to_all x2, waiting for transfers between devices, exchanged(): return lax.all_to_all(pieces, axis, 0, 0, tiled=True)  19.8 us
    all_to_all x2, starting transfers between devices, exchanged(): return lax.all_to_all(pieces, axis, 0, 0, tiled=True)  12.3 us
    pallas_call x1, Pallas kernels, grad_part(): pl.pallas_call(functools.partial(grad_kernel, shards, rows, most), out_sh...  8.89 us
    pallas_call x1, Pallas kernels, filter_part(): pl.pallas_call(functools.partial(filter_kernel, shards, rows, most, scale...  6.44 us
    ppermute x3, waiting for transfers between devices, shifted(): lax.ppermute(array, axis, [(i, (i + step) % count) for i in range(count)])  4.98 us
  transfers between devices with their start and end apart: 5, of which 5 were waited for; matrix products, arithmetic and copies ran while one was open for 0% of the time, Pallas kernels for 15%

profile of v4, /device:TPU:0, one launch (start us, length us, event | category | flops | bytes accessed | tf_op | source)
XLA Modules:
  0.0 59.4 jit_solution(17921906290614644278)
XLA Ops:
  0.6 0.6 collective-permute-start
  1.2 0.1 collective-permute-start.2
  1.3 2.4 %collective-permute-done.refs_1_.refs_3_ = bf16[1,128,4096]{2,1,0:T(8,128)(2,1)S(1)} collective-permute-done((bf16[1,128,4096]{2,1,0:T(8,128)(2,1)}, bf16[1,128,4096]{2,1,0:T(8,128)(2,1)S(1)}, u32[]{:S(2)}, u32[]{:S(2)}) %collective-permute-start) | collective-permute-done | bytes 1048608 | tf_op jit(solution)/shard_map/ppermute | solution.py:273
  3.7 1.5 %collective-permute-done.2.refs_1_ = bf16[1,128,4096]{2,1,0:T(8,128)(2,1)S(1)} collective-permute-done((bf16[1,128,4096]{2,1,0:T(8,128)(2,1)}, bf16[1,128,4096]{2,1,0:T(8,128)(2,1)S(1)}, u32[]{:S(2)}, u32[]{:S(2)}) %collective-permute-start.2) | collective-permute-done | bytes 1048608 | tf_op jit(solution)/shard_map/ppermute | solution.py:273
  5.2 6.4 %shard_map.122 = f32[16,136,128]{2,1,0:T(8,128)S(1)} custom-call(s32[1]{0:T(128)} %bitcast.me_ref, bf16[1,128,4096]{2,1,0:T(8,128)(2,1)} %refs_0_.3, bf16[1,128,4096]{2,1,0:T(8,128)(2,1)S(1)} %collective-permute-done.2.refs_1_, bf16[1,128,4096]{2,1,0:T(8,128)(2,1)} %refs_2_.3, bf16[1,128,4096]{2,1,0:T(8,128)(2,1)S(1)} %collective-permute-done.refs_1_.refs_3_, ...), custom_call_target="tpu_custom_call" | custom-call | flops 2550136832 | bytes 3145728 | tf_op jit(solution)/shard_map/pallas_call | solution.py:210
  11.6 0.9 %convert_element_type.11 = f16[16,136,128]{2,1,0:T(8,128)(2,1)} convert(f32[16,136,128]{2,1,0:T(8,128)S(1)} %shard_map.122) | non-fusion elementwise | flops 278528 | bytes 1671168 | tf_op jit(solution)/shard_map/convert_element_type | solution.py:321
  12.5 8.2 %all-to-all-start = ((f16[16,136,128]{2,1,0:T(8,128)(2,1)}), f16[16,136,128]{2,1,0:T(8,128)(2,1)S(1)}, u32[]{:S(2)}, u32[]{:S(2)}) async-start(f16[16,136,128]{2,1,0:T(8,128)(2,1)} %convert_element_type.11), calls=%async_computation | async-start | bytes 1114112 | tf_op jit(solution)/shard_map/all_to_all | solution.py:277
  20.7 15.9 %all-to-all-done = f16[16,136,128]{2,1,0:T(8,128)(2,1)S(1)} async-done(((f16[16,136,128]{2,1,0:T(8,128)(2,1)}), f16[16,136,128]{2,1,0:T(8,128)(2,1)S(1)}, u32[]{:S(2)}, u32[]{:S(2)}) %all-to-all-start) | async-done | bytes 557088 | tf_op jit(solution)/shard_map/all_to_all | solution.py:277
  36.7 0.1 convert_element_type.12
  36.8 0.1 fusion
  36.9 0.1 abs_reduce_fusion
  37.1 0.1 fusion.1
  37.2 0.1 select_convert_fusion
  37.3 0.1 copy.14
  37.4 0.9 %broadcast_in_dim.46 = f16[16,136,128]{2,1,0:T(8,128)(2,1)} broadcast(f16[136,128]{1,0:T(8,128)(2,1)S(1)} %copy.14), dimensions={1,2} | broadcast | bytes 591872 | tf_op jit(solution)/shard_map/broadcast_in_dim | solution.py:325
  38.3 4.1 %all-to-all-start.1 = ((f16[16,136,128]{2,1,0:T(8,128)(2,1)}), f16[16,136,128]{2,1,0:T(8,128)(2,1)S(1)}, u32[]{:S(2)}, u32[]{:S(2)}) async-start(f16[16,136,128]{2,1,0:T(8,128)(2,1)} %broadcast_in_dim.46), calls=%async_computation.1 | async-start | bytes 1114112 | tf_op jit(solution)/shard_map/all_to_all | solution.py:277
  42.4 8.9 %shard_map.121 = (bf16[1,128,2048]{2,1,0:T(8,128)(2,1)}, bf16[1,128,2048]{2,1,0:T(8,128)(2,1)}) custom-call(s32[1]{0:T(128)} %bitcast.me_ref, bf16[1,128,4096]{2,1,0:T(8,128)(2,1)} %refs_2_.3, bf16[1,128,4096]{2,1,0:T(8,128)(2,1)S(1)} %collective-permute-done.refs_1_.refs_3_, s32[1,256]{1,0:T(1,128)} %refs_4_.2, ...), custom_call_target="tpu_custom_call" | custom-call | flops 2952790016 | bytes 2621440 | tf_op jit(solution)/shard_map/pallas_call | solution.py:245
  51.3 0.0 copy-start.1
  51.3 0.0 collective-permute-start.1
  51.4 0.1 broadcast_in_dim.40
  51.5 0.9 %copy-done.1 = bf16[1,128,2048]{2,1,0:T(8,128)(2,1)S(1)} copy-done((bf16[1,128,2048]{2,1,0:T(8,128)(2,1)S(1)}, bf16[1,128,2048]{2,1,0:T(8,128)(2,1)}, u32[]{:S(2)}) %copy-start.1) | copy-done | bytes 524312
  52.4 1.1 %collective-permute-done.1 = bf16[1,128,2048]{2,1,0:T(8,128)(2,1)S(1)} collective-permute-done((bf16[1,128,2048]{2,1,0:T(8,128)(2,1)}, bf16[1,128,2048]{2,1,0:T(8,128)(2,1)S(1)}, u32[]{:S(2)}, u32[]{:S(2)}) %collective-permute-start.1) | collective-permute-done | bytes 524320 | tf_op jit(solution)/shard_map/ppermute | solution.py:273
  53.5 0.0 copy-start
  53.5 3.8 %all-to-all-done.1 = f16[16,136,128]{2,1,0:T(8,128)(2,1)S(1)} async-done(((f16[16,136,128]{2,1,0:T(8,128)(2,1)}), f16[16,136,128]{2,1,0:T(8,128)(2,1)S(1)}, u32[]{:S(2)}, u32[]{:S(2)}) %all-to-all-start.1) | async-done | bytes 557088 | tf_op jit(solution)/shard_map/all_to_all | solution.py:277
  57.4 0.1 convert_element_type.13
  57.5 0.2 slice_reduce_fusion
  57.7 1.1 %slice_multiply_fusion = f32[16,128,128]{2,1,0:T(8,128)} fusion(f32[16,136,128]{2,1,0:T(8,128)S(1)} %convert_element_type.13, f32[16,128]{1,0:T(8,128)S(1)} %bitcast.16), kind=kLoop, calls=%fused_computation | loop fusion | flops 262144 | bytes 2105344 | tf_op jit(solution)/shard_map/mul | solution.py:294
  58.8 0.0 copy-done
  58.8 0.7 %bitcast_multiply_fusion = f32[2048]{0:T(1024)} fusion(f32[2048]{0:T(1024)S(1)} %bitcast.18, f32[16]{0:T(128)S(1)} %slice_reduce_fusion), kind=kLoop, calls=%fused_computation.15 | loop fusion | flops 2048 | bytes 16448 | tf_op jit(solution)/shard_map/mul | solution.py:295
  (8 shorter events, 0.2 us)
Async XLA Ops:
  0.6 3.1 %collective-permute-start = (bf16[1,128,4096]{2,1,0:T(8,128)(2,1)}, bf16[1,128,4096]{2,1,0:T(8,128)(2,1)S(1)}, u32[]{:S(2)}, u32[]{:S(2)}) collective-permute-start(bf16[1,128,4096]{2,1,0:T(8,128)(2,1)} %refs_2_.3), channel_id=1, source_target_pairs={{0,1},{1,0},{2,3},{3,2},{4,5},{5,4},{6,7},{7,6},{8,9},{9,8},{10,11... | collective-permute-start | bytes 3145736 | tf_op jit(solution)/shard_map/ppermute | solution.py:273
  1.2 4.0 %collective-permute-start.2 = (bf16[1,128,4096]{2,1,0:T(8,128)(2,1)}, bf16[1,128,4096]{2,1,0:T(8,128)(2,1)S(1)}, u32[]{:S(2)}, u32[]{:S(2)}) collective-permute-start(bf16[1,128,4096]{2,1,0:T(8,128)(2,1)} %refs_0_.3), channel_id=1, source_target_pairs={{0,1},{1,0},{2,3},{3,2},{4,5},{5,4},{6,7},{7,6},{8,9},{9,8},{10,11... | collective-permute-start | bytes 3145736 | tf_op jit(solution)/shard_map/ppermute | solution.py:273
  12.5 24.2 %all-to-all-start = ((f16[16,136,128]{2,1,0:T(8,128)(2,1)}), f16[16,136,128]{2,1,0:T(8,128)(2,1)S(1)}, u32[]{:S(2)}, u32[]{:S(2)}) async-start(f16[16,136,128]{2,1,0:T(8,128)(2,1)} %convert_element_type.11), calls=%async_computation | async-start | bytes 1114112 | tf_op jit(solution)/shard_map/all_to_all | solution.py:277
  38.3 19.0 %all-to-all-start.1 = ((f16[16,136,128]{2,1,0:T(8,128)(2,1)}), f16[16,136,128]{2,1,0:T(8,128)(2,1)S(1)}, u32[]{:S(2)}, u32[]{:S(2)}) async-start(f16[16,136,128]{2,1,0:T(8,128)(2,1)} %broadcast_in_dim.46), calls=%async_computation.1 | async-start | bytes 1114112 | tf_op jit(solution)/shard_map/all_to_all | solution.py:277
  51.3 1.0 %copy-start.1 = (bf16[1,128,2048]{2,1,0:T(8,128)(2,1)S(1)}, bf16[1,128,2048]{2,1,0:T(8,128)(2,1)}, u32[]{:S(2)}) copy-start(bf16[1,128,2048]{2,1,0:T(8,128)(2,1)} %get-tuple-element.5) | copy-start | bytes 1572868
  51.3 2.2 %collective-permute-start.1 = (bf16[1,128,2048]{2,1,0:T(8,128)(2,1)}, bf16[1,128,2048]{2,1,0:T(8,128)(2,1)S(1)}, u32[]{:S(2)}, u32[]{:S(2)}) collective-permute-start(bf16[1,128,2048]{2,1,0:T(8,128)(2,1)} %get-tuple-element.6), channel_id=1, source_target_pairs={{0,1},{1,0},{2,3},{3,2},{4,5},{5,4},{6,7},{7,6},{8,9},{9,8},{10,11... | collective-permute-start | bytes 1572872 | tf_op jit(solution)/shard_map/ppermute | solution.py:273
  53.5 5.2 %copy-start = (bf16[1,128,4096]{2,1,0:T(8,128)(2,1)}, bf16[1,128,4096]{2,1,0:T(8,128)(2,1)S(1)}, u32[]{:S(2)}) copy-start(bf16[1,128,4096]{2,1,0:T(8,128)(2,1)S(1)} %constant_dynamic-update-slice_fusion) | copy-start | bytes 3145732

commit v5 on v4

--- a/solution.py
+++ b/solution.py
@@ -11,7 +11,7 @@
 LANES = 128
 STEP = 8
 TILES = 2
-SUBS = 2
+SUBS = 4
 BLOCK = LANES * TILES
 DOCS = 4
 TOP = 12.0
@@ -121,7 +121,7 @@
 
     order = sources(me_ref[0], shards)
     wide = SUBS * BLOCK
-    base = (me_ref[0] * pl.num_programs(0) + pl.program_id(0)) * wide
+    base = pl.program_id(0) * wide
     ahead = ahead_ref[...]
     for sub in range(u_all.shape[0]):
         u_full, g_full = u_all.at[sub], g_all.at[sub]
@@ -160,7 +160,7 @@
 
     order = sources(me_ref[0], shards)
     wide = SUBS * BLOCK
-    base = (me_ref[0] * pl.num_programs(0) + pl.program_id(0)) * wide
+    base = pl.program_id(0) * wide
     ahead = ahead_ref[...]
     for sub in range(g_all.shape[0]):
         g_full, total_ref = g_all.at[sub], total_all.at[sub]
@@ -288,12 +288,28 @@
     return jnp.concatenate([turned * power(TOP - exponents), note], axis=0)
 
 
+def whole_kernel(pieces_ref, taps_ref, skip_ref):
+    for k in range(pieces_ref.shape[0]):
+        note = pieces_ref[k, LANES:, :]
+        weights = power(note[:1] - TOP)
+        taps_ref[k * LANES : (k + 1) * LANES, :] = pieces_ref[k, :LANES, :] * weights
+        skip_ref[k : k + 1, :] = note[1:2] * weights[:, :1]
+
+
 def packed_whole(pieces):
-    pieces = pieces.astype(jnp.float32)
-    weights = power(pieces[:, LANES : LANES + 1, :] - TOP)
-    whole = pieces[:, :LANES, :] * weights
-    skip = pieces[:, LANES + 1, :] * weights[:, 0, :1]
-    return whole.reshape(-1, whole.shape[2]), skip.reshape(-1)
+    pieces = pltpu.with_memory_space_constraint(pieces.astype(jnp.float32), pltpu.VMEM)
+    count = pieces.shape[0]
+    whole, skip = pl.pallas_call(
+        whole_kernel,
+        grid=(count // STEP,),
+        in_specs=[pl.BlockSpec((STEP,) + pieces.shape[1:], lambda c: (c, 0, 0), memory_space=pltpu.VMEM)],
+        out_specs=[pl.BlockSpec((STEP * LANES, LANES), lambda c: (c, 0)), pl.BlockSpec((STEP, LANES), lambda c: (c, 0))],
+        out_shape=[
+            jax.ShapeDtypeStruct((count * LANES, LANES), jnp.float32),
+            jax.ShapeDtypeStruct((count, LANES), jnp.float32),
+        ],
+    )(pieces)
+    return whole, skip.reshape(-1)
 
 
 def plain_sum(parts, axis, count):
@@ -312,10 +328,15 @@
     width = inputs.shape[2] // count
     kernel = taps.shape[1]
     scale = 1.0 / (inputs.shape[0] * groups)
-    packed = width == groups * LANES and kernel == LANES
+    packed = width == groups * LANES and kernel == LANES and groups % STEP == 0
     held = lambda array: pltpu.with_memory_space_constraint(array, pltpu.VMEM) if packed else array
-    u_list = [inputs] + [held(shifted(inputs, "ctx", count, k)) for k in range(1, count)]
-    g_list = [cotangent] + [held(shifted(cotangent, "ctx", count, k)) for k in range(1, count)]
+
+    def wanted(array, step):
+        first = lax.rem(me[0] + step, count) * width
+        return held(shifted(lax.dynamic_slice_in_dim(array, first, width, 2), "ctx", count, step))
+
+    u_list = [inputs] + [wanted(inputs, k) for k in range(1, count)]
+    g_list = [cotangent] + [wanted(cotangent, k) for k in range(1, count)]
     parts = filter_part(me, u_list, g_list, segment_ids, kernel, scale, width, packed)
     if packed:
         pieces = exchanged(parts.astype(jnp.float16), "dp")

time: 59.8 us -> 58 us (0.970)
  other arithmetic: 3.23 us -> 1.45 us
  waiting for transfers between devices: 24.8 us -> 23.3 us
  local copies, waits for them, and re-layouts: 2.27 us -> 3.29 us
    ppermute x3, waiting for transfers between devices: 4.98 us -> 3.1 us  [shifted(): lax.ppermute(array, axis, [(i, (i + step) % count) for i in range(count)])]
    mul x2 -> x0, other arithmetic: 1.75 us -> none  [the longest x1 1.08 us: packed_whole(): whole = pieces[:, :LANES, :] * weights]
    dynamic_slice x0 -> x2, local copies, waits for them, and re-layouts: none -> 1.2 us  [wanted(): lax.dynamic_slice_in_dim(array, first, width, 2)]
    pallas_call x0 -> x1, Pallas kernels: none -> 1.05 us  [packed_whole(): pl.pallas_call(whole_kernel, grid=(count // STEP,), in_specs=[pl.BlockSpe...]
where the time goes in v5:
time: 58 us; the launch traced here: 57.6 us
  waiting for transfers between devices  23.3 us (40%)
  Pallas kernels  15.5 us (27%)
  starting transfers between devices  13.1 us (23%)
  local copies, waits for them, and re-layouts  3.29 us (6%)
  other arithmetic  1.45 us (2%)
  between operations  0.91 us (2%)
    all_to_all x2, waiting for transfers between devices, exchanged(): return lax.all_to_all(pieces, axis, 0, 0, tiled=True)  20.2 us
    all_to_all x2, starting transfers between devices, exchanged(): return lax.all_to_all(pieces, axis, 0, 0, tiled=True)  12.3 us
    pallas_call x1, Pallas kernels, grad_part(): pl.pallas_call(functools.partial(grad_kernel, shards, rows, most), out_sh...  8.48 us
    pallas_call x1, Pallas kernels, filter_part(): pl.pallas_call(functools.partial(filter_kernel, shards, rows, most, scale...  6 us
    ppermute x3, waiting for transfers between devices, shifted(): lax.ppermute(array, axis, [(i, (i + step) % count) for i in range(count)])  3.1 us
    dynamic_slice x2, local copies, waits for them, and re-layouts, wanted(): lax.dynamic_slice_in_dim(array, first, width, 2)  1.2 us
  transfers between devices with their start and end apart: 5, of which 5 were waited for; matrix products, arithmetic and copies ran while one was open for 0% of the time, Pallas kernels for 15%

profile of v5, /device:TPU:0, one launch (start us, length us, event | category | flops | bytes accessed | tf_op | source)
XLA Modules:
  0.0 57.6 jit_solution(13658397682959421544)
XLA Ops:
  0.6 0.0 copy-start.2
  0.7 1.2 %constant_dynamic-slice_fusion.1 = bf16[1,128,2048]{2,1,0:T(8,128)(2,1)S(1)} fusion(bf16[1,128,4096]{2,1,0:T(8,128)(2,1)} %refs_2_.3, s32[]{:T(128)S(6)} %select_n.12), kind=kLoop, calls=%fused_computation.13 | loop fusion | bytes 1048580 | tf_op jit(solution)/shard_map/dynamic_slice | solution.py:336
  1.8 0.6 collective-permute-start
  2.4 0.0 copy-done.2
  2.4 0.2 collective-permute-start.2
  2.6 1.3 %collective-permute-done.refs_1_.refs_3_ = bf16[1,128,2048]{2,1,0:T(8,128)(2,1)S(1)} collective-permute-done((bf16[1,128,2048]{2,1,0:T(8,128)(2,1)S(1)}, bf16[1,128,2048]{2,1,0:T(8,128)(2,1)S(1)}, u32[]{:S(2)}, u32[]{:S(2)}) %collective-permute-start) | collective-permute-done | bytes 524320 | tf_op jit(solution)/shard_map/ppermute | solution.py:273
  3.9 0.7 %collective-permute-done.2.refs_1_ = bf16[1,128,2048]{2,1,0:T(8,128)(2,1)S(1)} collective-permute-done((bf16[1,128,2048]{2,1,0:T(8,128)(2,1)S(1)}, bf16[1,128,2048]{2,1,0:T(8,128)(2,1)S(1)}, u32[]{:S(2)}, u32[]{:S(2)}) %collective-permute-start.2) | collective-permute-done | bytes 524320 | tf_op jit(solution)/shard_map/ppermute | solution.py:273
  4.7 6.0 %shard_map.122 = f32[16,136,128]{2,1,0:T(8,128)S(1)} custom-call(s32[1]{0:T(128)} %bitcast.me_ref, bf16[1,128,4096]{2,1,0:T(8,128)(2,1)} %refs_0_.3, bf16[1,128,2048]{2,1,0:T(8,128)(2,1)S(1)} %collective-permute-done.2.refs_1_, bf16[1,128,4096]{2,1,0:T(8,128)(2,1)} %refs_2_.3, bf16[1,128,2048]{2,1,0:T(8,128)(2,1)S(1)} %collective-permute-done.refs_1_.refs_3_, ...), custom_call_target="tpu_custom_call" | custom-call | flops 2550136832 | bytes 3145728 | tf_op jit(solution)/shard_map/pallas_call | solution.py:210
  10.7 0.9 %convert_element_type.11 = f16[16,136,128]{2,1,0:T(8,128)(2,1)} convert(f32[16,136,128]{2,1,0:T(8,128)S(1)} %shard_map.122) | non-fusion elementwise | flops 278528 | bytes 1671168 | tf_op jit(solution)/shard_map/convert_element_type | solution.py:342
  11.6 8.2 %all-to-all-start = ((f16[16,136,128]{2,1,0:T(8,128)(2,1)}), f16[16,136,128]{2,1,0:T(8,128)(2,1)S(1)}, u32[]{:S(2)}, u32[]{:S(2)}) async-start(f16[16,136,128]{2,1,0:T(8,128)(2,1)} %convert_element_type.11), calls=%async_computation | async-start | bytes 1114112 | tf_op jit(solution)/shard_map/all_to_all | solution.py:277
  19.8 16.0 %all-to-all-done = f16[16,136,128]{2,1,0:T(8,128)(2,1)S(1)} async-done(((f16[16,136,128]{2,1,0:T(8,128)(2,1)}), f16[16,136,128]{2,1,0:T(8,128)(2,1)S(1)}, u32[]{:S(2)}, u32[]{:S(2)}) %all-to-all-start) | async-done | bytes 557088 | tf_op jit(solution)/shard_map/all_to_all | solution.py:277
  35.8 0.1 convert_element_type.12
  35.9 0.1 fusion
  35.9 0.1 abs_reduce_fusion
  36.2 0.1 fusion.1
  36.3 0.1 select_convert_fusion
  36.4 0.1 copy.13
  36.5 0.9 %broadcast_in_dim.46 = f16[16,136,128]{2,1,0:T(8,128)(2,1)} broadcast(f16[136,128]{1,0:T(8,128)(2,1)S(1)} %copy.13), dimensions={1,2} | broadcast | bytes 591872 | tf_op jit(solution)/shard_map/broadcast_in_dim | solution.py:346
  37.4 4.1 %all-to-all-start.1 = ((f16[16,136,128]{2,1,0:T(8,128)(2,1)}), f16[16,136,128]{2,1,0:T(8,128)(2,1)S(1)}, u32[]{:S(2)}, u32[]{:S(2)}) async-start(f16[16,136,128]{2,1,0:T(8,128)(2,1)} %broadcast_in_dim.46), calls=%async_computation.1 | async-start | bytes 1114112 | tf_op jit(solution)/shard_map/all_to_all | solution.py:277
  41.5 8.5 %shard_map.121 = (bf16[1,128,2048]{2,1,0:T(8,128)(2,1)}, bf16[1,128,2048]{2,1,0:T(8,128)(2,1)}) custom-call(s32[1]{0:T(128)} %bitcast.me_ref, bf16[1,128,4096]{2,1,0:T(8,128)(2,1)} %refs_2_.3, bf16[1,128,2048]{2,1,0:T(8,128)(2,1)S(1)} %collective-permute-done.refs_1_.refs_3_, s32[1,256]{1,0:T(1,128)} %refs_4_.2, ...), custom_call_target="tpu_custom_call" | custom-call | flops 2952790016 | bytes 2621440 | tf_op jit(solution)/shard_map/pallas_call | solution.py:245
  50.0 0.0 copy-start.1
  50.0 0.0 collective-permute-start.1
  50.0 0.1 broadcast_in_dim.40
  50.1 0.9 %copy-done.1 = bf16[1,128,2048]{2,1,0:T(8,128)(2,1)S(1)} copy-done((bf16[1,128,2048]{2,1,0:T(8,128)(2,1)S(1)}, bf16[1,128,2048]{2,1,0:T(8,128)(2,1)}, u32[]{:S(2)}) %copy-start.1) | copy-done | bytes 524312
  51.1 1.1 %collective-permute-done.1 = bf16[1,128,2048]{2,1,0:T(8,128)(2,1)S(1)} collective-permute-done((bf16[1,128,2048]{2,1,0:T(8,128)(2,1)}, bf16[1,128,2048]{2,1,0:T(8,128)(2,1)S(1)}, u32[]{:S(2)}, u32[]{:S(2)}) %collective-permute-start.1) | collective-permute-done | bytes 524320 | tf_op jit(solution)/shard_map/ppermute | solution.py:273
  52.2 0.0 copy-start
  52.2 4.2 %all-to-all-done.1 = f16[16,136,128]{2,1,0:T(8,128)(2,1)S(1)} async-done(((f16[16,136,128]{2,1,0:T(8,128)(2,1)}), f16[16,136,128]{2,1,0:T(8,128)(2,1)S(1)}, u32[]{:S(2)}, u32[]{:S(2)}) %all-to-all-start.1) | async-done | bytes 557088 | tf_op jit(solution)/shard_map/all_to_all | solution.py:277
  56.4 0.1 convert_element_type.13.pieces_ref
  56.5 1.0 %shard_map.123 = (f32[2048,128]{1,0:T(8,128)}, f32[16,128]{1,0:T(8,128)}) custom-call(f32[16,136,128]{2,1,0:T(8,128)S(1)} %convert_element_type.13.pieces_ref), custom_call_target="tpu_custom_call" | custom-call | tf_op jit(solution)/shard_map/pallas_call | solution.py:302
  57.6 0.0 copy-done
  (8 shorter events, 0.2 us)
Async XLA Ops:
  0.6 1.7 %copy-start.2 = (bf16[1,128,4096]{2,1,0:T(8,128)(2,1)S(1)}, bf16[1,128,4096]{2,1,0:T(8,128)(2,1)}, u32[]{:S(2)}) copy-start(bf16[1,128,4096]{2,1,0:T(8,128)(2,1)} %refs_0_.3) | copy-start | bytes 3145732
  1.8 2.1 %collective-permute-start = (bf16[1,128,2048]{2,1,0:T(8,128)(2,1)S(1)}, bf16[1,128,2048]{2,1,0:T(8,128)(2,1)S(1)}, u32[]{:S(2)}, u32[]{:S(2)}) collective-permute-start(bf16[1,128,2048]{2,1,0:T(8,128)(2,1)S(1)} %constant_dynamic-slice_fusion.1), channel_id=1, source_target_pairs={{0,1},{1,0},{2,3},{3,2},{4,5},{5,4},{6,7},{7,6},{8,9},{9,8},{10,11... | collective-permute-start | bytes 1572872 | tf_op jit(solution)/shard_map/ppermute | solution.py:273
  2.4 2.2 %collective-permute-start.2 = (bf16[1,128,2048]{2,1,0:T(8,128)(2,1)S(1)}, bf16[1,128,2048]{2,1,0:T(8,128)(2,1)S(1)}, u32[]{:S(2)}, u32[]{:S(2)}) collective-permute-start(bf16[1,128,2048]{2,1,0:T(8,128)(2,1)S(1)} %constant_dynamic-slice_fusion), channel_id=1, source_target_pairs={{0,1},{1,0},{2,3},{3,2},{4,5},{5,4},{6,7},{7,6},{8,9},{9,8},{10,11... | collective-permute-start | bytes 1572872 | tf_op jit(solution)/shard_map/ppermute | solution.py:273
  11.6 24.2 %all-to-all-start = ((f16[16,136,128]{2,1,0:T(8,128)(2,1)}), f16[16,136,128]{2,1,0:T(8,128)(2,1)S(1)}, u32[]{:S(2)}, u32[]{:S(2)}) async-start(f16[16,136,128]{2,1,0:T(8,128)(2,1)} %convert_element_type.11), calls=%async_computation | async-start | bytes 1114112 | tf_op jit(solution)/shard_map/all_to_all | solution.py:277
  37.4 19.0 %all-to-all-start.1 = ((f16[16,136,128]{2,1,0:T(8,128)(2,1)}), f16[16,136,128]{2,1,0:T(8,128)(2,1)S(1)}, u32[]{:S(2)}, u32[]{:S(2)}) async-start(f16[16,136,128]{2,1,0:T(8,128)(2,1)} %broadcast_in_dim.46), calls=%async_computation.1 | async-start | bytes 1114112 | tf_op jit(solution)/shard_map/all_to_all | solution.py:277
  50.0 1.0 %copy-start.1 = (bf16[1,128,2048]{2,1,0:T(8,128)(2,1)S(1)}, bf16[1,128,2048]{2,1,0:T(8,128)(2,1)}, u32[]{:S(2)}) copy-start(bf16[1,128,2048]{2,1,0:T(8,128)(2,1)} %get-tuple-element.7) | copy-start | bytes 1572868
  50.0 2.2 %collective-permute-start.1 = (bf16[1,128,2048]{2,1,0:T(8,128)(2,1)}, bf16[1,128,2048]{2,1,0:T(8,128)(2,1)S(1)}, u32[]{:S(2)}, u32[]{:S(2)}) collective-permute-start(bf16[1,128,2048]{2,1,0:T(8,128)(2,1)} %get-tuple-element.8), channel_id=1, source_target_pairs={{0,1},{1,0},{2,3},{3,2},{4,5},{5,4},{6,7},{7,6},{8,9},{9,8},{10,11... | collective-permute-start | bytes 1572872 | tf_op jit(solution)/shard_map/ppermute | solution.py:273
  52.2 5.4 %copy-start = (bf16[1,128,4096]{2,1,0:T(8,128)(2,1)}, bf16[1,128,4096]{2,1,0:T(8,128)(2,1)S(1)}, u32[]{:S(2)}) copy-start(bf16[1,128,4096]{2,1,0:T(8,128)(2,1)S(1)} %constant_dynamic-update-slice_fusion) | copy-start | bytes 3145732

commit v6 on v5

--- a/solution.py
+++ b/solution.py
@@ -17,6 +17,7 @@
 TOP = 12.0
 NOTE = STEP
 TINY = 1e-30
+LONG = 2
 
 
 def up(value, unit):
@@ -63,14 +64,22 @@
     return jnp.dot(table, jnp.concatenate(high + low + high, axis=0), preferred_element_type=jnp.float32)
 
 
-def documents(ids_ref, info_ref):
+def documents(ids_ref, info_ref, ranked=False):
     ids = ids_ref[...]
     begin = jnp.int32(0)
+    begins, counts = [], []
     for doc in range(DOCS):
         count = jnp.sum(jnp.where(ids == doc, 1.0, 0.0)).astype(jnp.int32)
-        info_ref[doc] = begin
-        info_ref[DOCS + doc] = count
+        begins.append(begin)
+        counts.append(count)
         begin = begin + count
+    for doc in range(DOCS):
+        slot = doc
+        if ranked:
+            ahead = [counts[k] >= counts[doc] if k < doc else counts[k] > counts[doc] for k in range(DOCS) if k != doc]
+            slot = sum(jnp.where(flag, 1, 0) for flag in ahead)
+        info_ref[slot] = begins[doc]
+        info_ref[DOCS + slot] = counts[doc]
 
 
 def widen(refs, shards, rows, full_ref, sub, base):
@@ -110,31 +119,42 @@
 def filter_kernel(shards, rows, most, scale, packed, me_ref, *refs):
     u_refs = refs[:shards]
     g_refs = refs[shards : 2 * shards]
-    ids_ref, ahead_ref, back_ref, out_ref, info_ref, u_all, g_all = refs[2 * shards :]
+    ids_ref, ahead_ref, back_ref, brief_ahead_ref, brief_back_ref = refs[2 * shards : 2 * shards + 5]
+    out_ref, info_ref, u_all, g_all = refs[2 * shards + 5 :]
     length = shards * rows
     kernel = LANES
 
     @pl.when(pl.program_id(0) == 0)
     def _():
-        documents(ids_ref, info_ref)
+        documents(ids_ref, info_ref, ranked=True)
         u_all[:, :, length:, :] = jnp.zeros(u_all.shape[:2] + (most, LANES), jnp.float32)
 
     order = sources(me_ref[0], shards)
     wide = SUBS * BLOCK
     base = pl.program_id(0) * wide
-    ahead = ahead_ref[...]
+    far = base + me_ref[0] * (pl.num_programs(0) * wide)
     for sub in range(u_all.shape[0]):
         u_full, g_full = u_all.at[sub], g_all.at[sub]
         widen(u_refs, order, rows, u_full, sub, base)
-        widen(g_refs, order, rows, g_full, sub, base)
-        product = None
-        for doc in range(DOCS):
-            begin = info_ref[doc]
-            g_wave = spectrum(ahead, window(g_full, begin, most, info_ref[DOCS + doc]))
-            u_wave = spectrum(ahead, window(u_full, begin, most))
-            more = against(g_wave, u_wave)
-            product = more if product is None else [old + new for old, new in zip(product, more)]
-        taps = inverse(back_ref[:kernel, :], product) * scale
+        widen(g_refs, order, rows, g_full, sub, far)
+        taps = 0.0
+        for slots, reach, ahead, back_at in (
+            (range(LONG), most, ahead_ref[...], back_ref),
+            (range(LONG, DOCS), most // 2, brief_ahead_ref[...], brief_back_ref),
+        ):
+            product = None
+            for slot in slots:
+                begin = info_ref[slot]
+                g_wave = spectrum(ahead, window(g_full, begin, reach, info_ref[DOCS + slot]))
+                u_wave = spectrum(ahead, window(u_full, begin, reach))
+                more = against(g_wave, u_wave)
+                product = more if product is None else [old + new for old, new in zip(product, more)]
+            lags = min(kernel, reach)
+            part = inverse(back_at[:lags, :], product)
+            if lags < kernel:
+                part = jnp.concatenate([part, jnp.zeros((kernel - lags, BLOCK), jnp.float32)], axis=0)
+            taps = taps + part
+        taps = taps * scale
         if packed:
             exponent = exponent_of(jnp.max(jnp.abs(taps), axis=0, keepdims=True))
             taps = taps * power(TOP - exponent)
@@ -161,10 +181,11 @@
     order = sources(me_ref[0], shards)
     wide = SUBS * BLOCK
     base = pl.program_id(0) * wide
+    far = base + me_ref[0] * (pl.num_programs(0) * wide)
     ahead = ahead_ref[...]
     for sub in range(g_all.shape[0]):
         g_full, total_ref = g_all.at[sub], total_all.at[sub]
-        widen(g_refs, order, rows, g_full, sub, base)
+        widen(g_refs, order, rows, g_full, sub, far)
         taps = taps_ref[sub * BLOCK : (sub + 1) * BLOCK, :]
         h_wave = lax.dot_general(
             head_ref[...],
@@ -195,7 +216,8 @@
     most = length // 2
     wide = SUBS * BLOCK
     blocks = width // wide
-    ahead, back = tables(most, kernel)
+    fixed_tables = tables(most, kernel) + tables(most // 2, min(kernel, most // 2))
+    ahead, back = fixed_tables[:2]
     data = pl.BlockSpec((1, rows, wide), lambda c, me_ref: (0, 0, me_ref[0] * blocks + c))
     got = pl.BlockSpec(memory_space=pltpu.VMEM)
     fixed = lambda array: pl.BlockSpec(array.shape, lambda c, me_ref: (0, 0))
@@ -213,7 +235,7 @@
         grid_spec=pltpu.PrefetchScalarGridSpec(
             num_scalar_prefetch=1,
             grid=(blocks,),
-            in_specs=([data] + [got] * (shards - 1)) * 2 + [fixed(ids), fixed(ahead), fixed(back)],
+            in_specs=([data] + [got] * (shards - 1)) * 2 + [fixed(ids)] + [fixed(table) for table in fixed_tables],
             out_specs=out_spec,
             scratch_shapes=[
                 pltpu.SMEM((2 * DOCS,), jnp.int32),
@@ -226,7 +248,7 @@
             bytes_accessed=width * (4 * length + 4 * kernel),
             transcendentals=0,
         ),
-    )(me, *u_list, *g_list, ids, jnp.asarray(ahead), jnp.asarray(back))
+    )(me, *u_list, *g_list, ids, *map(jnp.asarray, fixed_tables))
 
 
 def grad_part(me, g_list, ids, taps, skip_gain, width):
@@ -336,7 +358,7 @@
         return held(shifted(lax.dynamic_slice_in_dim(array, first, width, 2), "ctx", count, step))
 
     u_list = [inputs] + [wanted(inputs, k) for k in range(1, count)]
-    g_list = [cotangent] + [wanted(cotangent, k) for k in range(1, count)]
+    g_list = [cotangent] + [held(shifted(cotangent, "ctx", count, k)) for k in range(1, count)]
     parts = filter_part(me, u_list, g_list, segment_ids, kernel, scale, width, packed)
     if packed:
         pieces = exchanged(parts.astype(jnp.float16), "dp")

time: 58 us -> 57.7 us (level)
    dynamic_slice x2 -> x1, local copies, waits for them, and re-layouts: 1.2 us -> 1.08 us  [wanted(): lax.dynamic_slice_in_dim(array, first, width, 2)]
  transfers between devices with their start and end apart: 5 -> 5, of which waited for: 5 -> 4; matrix products, arithmetic and copies ran while one was open for 0% -> 2% of each run, Pallas kernels for 15% -> 15%
where the time goes in v6:
time: 57.7 us; the launch traced here: 57.2 us
  waiting for transfers between devices  23.3 us (40%)
  Pallas kernels  15.5 us (27%)
  starting transfers between devices  13 us (23%)
  local copies, waits for them, and re-layouts  3.16 us (5%)
  other arithmetic  1.45 us (3%)
  between operations  0.88 us (2%)
    all_to_all x2, waiting for transfers between devices, exchanged(): return lax.all_to_all(pieces, axis, 0, 0, tiled=True)  20.2 us
    all_to_all x2, starting transfers between devices, exchanged(): return lax.all_to_all(pieces, axis, 0, 0, tiled=True)  12.3 us
    pallas_call x1, Pallas kernels, grad_part(): pl.pallas_call(functools.partial(grad_kernel, shards, rows, most), out_sh...  8.48 us
    pallas_call x1, Pallas kernels, filter_part(): pl.pallas_call(functools.partial(filter_kernel, shards, rows, most, scale...  5.95 us
    ppermute x3, waiting for transfers between devices, shifted(): lax.ppermute(array, axis, [(i, (i + step) % count) for i in range(count)])  3.13 us
  transfers between devices with their start and end apart: 5, of which 4 were waited for; matrix products, arithmetic and copies ran while one was open for 2% of the time, Pallas kernels for 15%

profile of v6, /device:TPU:0, one launch (start us, length us, event | category | flops | bytes accessed | tf_op | source)
XLA Modules:
  0.0 57.2 jit_solution(10135773486767529141)
XLA Ops:
  0.6 0.6 collective-permute-start
  1.2 1.1 %constant_dynamic-slice_fusion = bf16[1,128,2048]{2,1,0:T(8,128)(2,1)S(1)} fusion(bf16[1,128,4096]{2,1,0:T(8,128)(2,1)} %refs_0_.3, s32[]{:T(128)S(6)} %select_n.12), kind=kLoop, calls=%fused_computation.10 | loop fusion | bytes 1048580 | tf_op jit(solution)/shard_map/dynamic_slice | solution.py:358
  2.3 0.1 collective-permute-start.2
  2.4 2.1 %collective-permute-done.2.refs_1_ = bf16[1,128,2048]{2,1,0:T(8,128)(2,1)S(1)} collective-permute-done((bf16[1,128,2048]{2,1,0:T(8,128)(2,1)S(1)}, bf16[1,128,2048]{2,1,0:T(8,128)(2,1)S(1)}, u32[]{:S(2)}, u32[]{:S(2)}) %collective-permute-start.2) | collective-permute-done | bytes 524320 | tf_op jit(solution)/shard_map/ppermute | solution.py:295
  4.4 0.0 collective-permute-done.refs_1_.refs_3_
  4.4 5.9 %shard_map.140 = f32[16,136,128]{2,1,0:T(8,128)S(1)} custom-call(s32[1]{0:T(128)} %bitcast.me_ref, bf16[1,128,4096]{2,1,0:T(8,128)(2,1)} %refs_0_.3, bf16[1,128,2048]{2,1,0:T(8,128)(2,1)S(1)} %collective-permute-done.2.refs_1_, bf16[1,128,4096]{2,1,0:T(8,128)(2,1)} %refs_2_.3, bf16[1,128,4096]{2,1,0:T(8,128)(2,1)S(1)} %collective-permute-done.refs_1_.refs_3_, ...), custom_call_target="tpu_custom_call" | custom-call | flops 2550136832 | bytes 3145728 | tf_op jit(solution)/shard_map/pallas_call | solution.py:232
  10.4 0.9 %convert_element_type.11 = f16[16,136,128]{2,1,0:T(8,128)(2,1)} convert(f32[16,136,128]{2,1,0:T(8,128)S(1)} %shard_map.140) | non-fusion elementwise | flops 278528 | bytes 1671168 | tf_op jit(solution)/shard_map/convert_element_type | solution.py:364
  11.3 8.2 %all-to-all-start = ((f16[16,136,128]{2,1,0:T(8,128)(2,1)}), f16[16,136,128]{2,1,0:T(8,128)(2,1)S(1)}, u32[]{:S(2)}, u32[]{:S(2)}) async-start(f16[16,136,128]{2,1,0:T(8,128)(2,1)} %convert_element_type.11), calls=%async_computation | async-start | bytes 1114112 | tf_op jit(solution)/shard_map/all_to_all | solution.py:299
  19.5 15.9 %all-to-all-done = f16[16,136,128]{2,1,0:T(8,128)(2,1)S(1)} async-done(((f16[16,136,128]{2,1,0:T(8,128)(2,1)}), f16[16,136,128]{2,1,0:T(8,128)(2,1)S(1)}, u32[]{:S(2)}, u32[]{:S(2)}) %all-to-all-start) | async-done | bytes 557088 | tf_op jit(solution)/shard_map/all_to_all | solution.py:299
  35.4 0.1 convert_element_type.12
  35.5 0.1 fusion
  35.6 0.1 abs_reduce_fusion
  35.9 0.1 fusion.1
  35.9 0.1 select_convert_fusion
  36.1 0.1 copy.15
  36.2 0.9 %broadcast_in_dim.46 = f16[16,136,128]{2,1,0:T(8,128)(2,1)} broadcast(f16[136,128]{1,0:T(8,128)(2,1)S(1)} %copy.15), dimensions={1,2} | broadcast | bytes 591872 | tf_op jit(solution)/shard_map/broadcast_in_dim | solution.py:368
  37.1 4.1 %all-to-all-start.1 = ((f16[16,136,128]{2,1,0:T(8,128)(2,1)}), f16[16,136,128]{2,1,0:T(8,128)(2,1)S(1)}, u32[]{:S(2)}, u32[]{:S(2)}) async-start(f16[16,136,128]{2,1,0:T(8,128)(2,1)} %broadcast_in_dim.46), calls=%async_computation.1 | async-start | bytes 1114112 | tf_op jit(solution)/shard_map/all_to_all | solution.py:299
  41.2 8.5 %shard_map.139 = (bf16[1,128,2048]{2,1,0:T(8,128)(2,1)}, bf16[1,128,2048]{2,1,0:T(8,128)(2,1)}) custom-call(s32[1]{0:T(128)} %bitcast.me_ref, bf16[1,128,4096]{2,1,0:T(8,128)(2,1)} %refs_2_.3, bf16[1,128,4096]{2,1,0:T(8,128)(2,1)S(1)} %collective-permute-done.refs_1_.refs_3_, s32[1,256]{1,0:T(1,128)} %refs_4_.2, ...), custom_call_target="tpu_custom_call" | custom-call | flops 2952790016 | bytes 2621440 | tf_op jit(solution)/shard_map/pallas_call | solution.py:267
  49.7 0.0 copy-start.1
  49.7 0.0 collective-permute-start.1
  49.7 0.1 broadcast_in_dim.40
  49.8 0.9 %copy-done.1 = bf16[1,128,2048]{2,1,0:T(8,128)(2,1)S(1)} copy-done((bf16[1,128,2048]{2,1,0:T(8,128)(2,1)S(1)}, bf16[1,128,2048]{2,1,0:T(8,128)(2,1)}, u32[]{:S(2)}) %copy-start.1) | copy-done | bytes 524312
  50.8 1.1 %collective-permute-done.1 = bf16[1,128,2048]{2,1,0:T(8,128)(2,1)S(1)} collective-permute-done((bf16[1,128,2048]{2,1,0:T(8,128)(2,1)}, bf16[1,128,2048]{2,1,0:T(8,128)(2,1)S(1)}, u32[]{:S(2)}, u32[]{:S(2)}) %collective-permute-start.1) | collective-permute-done | bytes 524320 | tf_op jit(solution)/shard_map/ppermute | solution.py:295
  51.9 0.0 copy-start
  51.9 4.2 %all-to-all-done.1 = f16[16,136,128]{2,1,0:T(8,128)(2,1)S(1)} async-done(((f16[16,136,128]{2,1,0:T(8,128)(2,1)}), f16[16,136,128]{2,1,0:T(8,128)(2,1)S(1)}, u32[]{:S(2)}, u32[]{:S(2)}) %all-to-all-start.1) | async-done | bytes 557088 | tf_op jit(solution)/shard_map/all_to_all | solution.py:299
  56.1 0.1 convert_element_type.13.pieces_ref
  56.2 1.0 %shard_map.141 = (f32[2048,128]{1,0:T(8,128)}, f32[16,128]{1,0:T(8,128)}) custom-call(f32[16,136,128]{2,1,0:T(8,128)S(1)} %convert_element_type.13.pieces_ref), custom_call_target="tpu_custom_call" | custom-call | tf_op jit(solution)/shard_map/pallas_call | solution.py:324
  57.2 0.0 copy-done
  (7 shorter events, 0.2 us)
Async XLA Ops:
  0.6 3.8 %collective-permute-start = (bf16[1,128,4096]{2,1,0:T(8,128)(2,1)}, bf16[1,128,4096]{2,1,0:T(8,128)(2,1)S(1)}, u32[]{:S(2)}, u32[]{:S(2)}) collective-permute-start(bf16[1,128,4096]{2,1,0:T(8,128)(2,1)} %refs_2_.3), channel_id=1, source_target_pairs={{0,1},{1,0},{2,3},{3,2},{4,5},{5,4},{6,7},{7,6},{8,9},{9,8},{10,11... | collective-permute-start | bytes 3145736 | tf_op jit(solution)/shard_map/ppermute | solution.py:295
  2.3 2.2 %collective-permute-start.2 = (bf16[1,128,2048]{2,1,0:T(8,128)(2,1)S(1)}, bf16[1,128,2048]{2,1,0:T(8,128)(2,1)S(1)}, u32[]{:S(2)}, u32[]{:S(2)}) collective-permute-start(bf16[1,128,2048]{2,1,0:T(8,128)(2,1)S(1)} %constant_dynamic-slice_fusion), channel_id=1, source_target_pairs={{0,1},{1,0},{2,3},{3,2},{4,5},{5,4},{6,7},{7,6},{8,9},{9,8},{10,11... | collective-permute-start | bytes 1572872 | tf_op jit(solution)/shard_map/ppermute | solution.py:295
  11.3 24.2 %all-to-all-start = ((f16[16,136,128]{2,1,0:T(8,128)(2,1)}), f16[16,136,128]{2,1,0:T(8,128)(2,1)S(1)}, u32[]{:S(2)}, u32[]{:S(2)}) async-start(f16[16,136,128]{2,1,0:T(8,128)(2,1)} %convert_element_type.11), calls=%async_computation | async-start | bytes 1114112 | tf_op jit(solution)/shard_map/all_to_all | solution.py:299
  37.1 19.0 %all-to-all-start.1 = ((f16[16,136,128]{2,1,0:T(8,128)(2,1)}), f16[16,136,128]{2,1,0:T(8,128)(2,1)S(1)}, u32[]{:S(2)}, u32[]{:S(2)}) async-start(f16[16,136,128]{2,1,0:T(8,128)(2,1)} %broadcast_in_dim.46), calls=%async_computation.1 | async-start | bytes 1114112 | tf_op jit(solution)/shard_map/all_to_all | solution.py:299
  49.7 1.0 %copy-start.1 = (bf16[1,128,2048]{2,1,0:T(8,128)(2,1)S(1)}, bf16[1,128,2048]{2,1,0:T(8,128)(2,1)}, u32[]{:S(2)}) copy-start(bf16[1,128,2048]{2,1,0:T(8,128)(2,1)} %get-tuple-element.7) | copy-start | bytes 1572868
  49.7 2.2 %collective-permute-start.1 = (bf16[1,128,2048]{2,1,0:T(8,128)(2,1)}, bf16[1,128,2048]{2,1,0:T(8,128)(2,1)S(1)}, u32[]{:S(2)}, u32[]{:S(2)}) collective-permute-start(bf16[1,128,2048]{2,1,0:T(8,128)(2,1)} %get-tuple-element.8), channel_id=1, source_target_pairs={{0,1},{1,0},{2,3},{3,2},{4,5},{5,4},{6,7},{7,6},{8,9},{9,8},{10,11... | collective-permute-start | bytes 1572872 | tf_op jit(solution)/shard_map/ppermute | solution.py:295
  51.9 5.4 %copy-start = (bf16[1,128,4096]{2,1,0:T(8,128)(2,1)}, bf16[1,128,4096]{2,1,0:T(8,128)(2,1)S(1)}, u32[]{:S(2)}) copy-start(bf16[1,128,4096]{2,1,0:T(8,128)(2,1)S(1)} %constant_dynamic-update-slice_fusion) | copy-start | bytes 3145732

commit v7 on v6

--- a/solution.py
+++ b/solution.py
@@ -134,9 +134,10 @@
     base = pl.program_id(0) * wide
     far = base + me_ref[0] * (pl.num_programs(0) * wide)
     for sub in range(u_all.shape[0]):
+        widen(u_refs, order, rows, u_all.at[sub], sub, base)
+        widen(g_refs, order, rows, g_all.at[sub], sub, far)
+    for sub in range(u_all.shape[0]):
         u_full, g_full = u_all.at[sub], g_all.at[sub]
-        widen(u_refs, order, rows, u_full, sub, base)
-        widen(g_refs, order, rows, g_full, sub, far)
         taps = 0.0
         for slots, reach, ahead, back_at in (
             (range(LONG), most, ahead_ref[...], back_ref),

time: 57.7 us -> 57.7 us (level)
  no operation moved by 1% of the time
where the time goes in v7:
time: 57.7 us; the launch traced here: 57.2 us
  waiting for transfers between devices  23.3 us (40%)
  Pallas kernels  15.5 us (27%)
  starting transfers between devices  13 us (23%)
  local copies, waits for them, and re-layouts  3.16 us (5%)
  other arithmetic  1.45 us (3%)
  between operations  0.88 us (2%)
    all_to_all x2, waiting for transfers between devices, exchanged(): return lax.all_to_all(pieces, axis, 0, 0, tiled=True)  20.2 us
    all_to_all x2, starting transfers between devices, exchanged(): return lax.all_to_all(pieces, axis, 0, 0, tiled=True)  12.3 us
    pallas_call x1, Pallas kernels, grad_part(): pl.pallas_call(functools.partial(grad_kernel, shards, rows, most), out_sh...  8.47 us
    pallas_call x1, Pallas kernels, filter_part(): pl.pallas_call(functools.partial(filter_kernel, shards, rows, most, scale...  5.94 us
    ppermute x3, waiting for transfers between devices, shifted(): lax.ppermute(array, axis, [(i, (i + step) % count) for i in range(count)])  3.13 us
  transfers between devices with their start and end apart: 5, of which 4 were waited for; matrix products, arithmetic and copies ran while one was open for 2% of the time, Pallas kernels for 15%

profile of v7, /device:TPU:0, one launch (start us, length us, event | category | flops | bytes accessed | tf_op | source)
XLA Modules:
  0.0 57.2 jit_solution(8070931856032168250)
XLA Ops:
  0.6 0.6 collective-permute-start
  1.2 1.1 %constant_dynamic-slice_fusion = bf16[1,128,2048]{2,1,0:T(8,128)(2,1)S(1)} fusion(bf16[1,128,4096]{2,1,0:T(8,128)(2,1)} %refs_0_.3, s32[]{:T(128)S(6)} %select_n.12), kind=kLoop, calls=%fused_computation.10 | loop fusion | bytes 1048580 | tf_op jit(solution)/shard_map/dynamic_slice | solution.py:359
  2.3 0.1 collective-permute-start.2
  2.4 2.1 %collective-permute-done.2.refs_1_ = bf16[1,128,2048]{2,1,0:T(8,128)(2,1)S(1)} collective-permute-done((bf16[1,128,2048]{2,1,0:T(8,128)(2,1)S(1)}, bf16[1,128,2048]{2,1,0:T(8,128)(2,1)S(1)}, u32[]{:S(2)}, u32[]{:S(2)}) %collective-permute-start.2) | collective-permute-done | bytes 524320 | tf_op jit(solution)/shard_map/ppermute | solution.py:296
  4.4 0.0 collective-permute-done.refs_1_.refs_3_
  4.4 5.9 %shard_map.140 = f32[16,136,128]{2,1,0:T(8,128)S(1)} custom-call(s32[1]{0:T(128)} %bitcast.me_ref, bf16[1,128,4096]{2,1,0:T(8,128)(2,1)} %refs_0_.3, bf16[1,128,2048]{2,1,0:T(8,128)(2,1)S(1)} %collective-permute-done.2.refs_1_, bf16[1,128,4096]{2,1,0:T(8,128)(2,1)} %refs_2_.3, bf16[1,128,4096]{2,1,0:T(8,128)(2,1)S(1)} %collective-permute-done.refs_1_.refs_3_, ...), custom_call_target="tpu_custom_call" | custom-call | flops 2550136832 | bytes 3145728 | tf_op jit(solution)/shard_map/pallas_call | solution.py:233
  10.4 0.9 %convert_element_type.11 = f16[16,136,128]{2,1,0:T(8,128)(2,1)} convert(f32[16,136,128]{2,1,0:T(8,128)S(1)} %shard_map.140) | non-fusion elementwise | flops 278528 | bytes 1671168 | tf_op jit(solution)/shard_map/convert_element_type | solution.py:365
  11.3 8.2 %all-to-all-start = ((f16[16,136,128]{2,1,0:T(8,128)(2,1)}), f16[16,136,128]{2,1,0:T(8,128)(2,1)S(1)}, u32[]{:S(2)}, u32[]{:S(2)}) async-start(f16[16,136,128]{2,1,0:T(8,128)(2,1)} %convert_element_type.11), calls=%async_computation | async-start | bytes 1114112 | tf_op jit(solution)/shard_map/all_to_all | solution.py:300
  19.5 15.9 %all-to-all-done = f16[16,136,128]{2,1,0:T(8,128)(2,1)S(1)} async-done(((f16[16,136,128]{2,1,0:T(8,128)(2,1)}), f16[16,136,128]{2,1,0:T(8,128)(2,1)S(1)}, u32[]{:S(2)}, u32[]{:S(2)}) %all-to-all-start) | async-done | bytes 557088 | tf_op jit(solution)/shard_map/all_to_all | solution.py:300
  35.4 0.1 convert_element_type.12
  35.5 0.1 fusion
  35.6 0.1 abs_reduce_fusion
  35.8 0.1 fusion.1
  35.9 0.1 select_convert_fusion
  36.1 0.1 copy.15
  36.2 0.9 %broadcast_in_dim.46 = f16[16,136,128]{2,1,0:T(8,128)(2,1)} broadcast(f16[136,128]{1,0:T(8,128)(2,1)S(1)} %copy.15), dimensions={1,2} | broadcast | bytes 591872 | tf_op jit(solution)/shard_map/broadcast_in_dim | solution.py:369
  37.1 4.1 %all-to-all-start.1 = ((f16[16,136,128]{2,1,0:T(8,128)(2,1)}), f16[16,136,128]{2,1,0:T(8,128)(2,1)S(1)}, u32[]{:S(2)}, u32[]{:S(2)}) async-start(f16[16,136,128]{2,1,0:T(8,128)(2,1)} %broadcast_in_dim.46), calls=%async_computation.1 | async-start | bytes 1114112 | tf_op jit(solution)/shard_map/all_to_all | solution.py:300
  41.2 8.5 %shard_map.139 = (bf16[1,128,2048]{2,1,0:T(8,128)(2,1)}, bf16[1,128,2048]{2,1,0:T(8,128)(2,1)}) custom-call(s32[1]{0:T(128)} %bitcast.me_ref, bf16[1,128,4096]{2,1,0:T(8,128)(2,1)} %refs_2_.3, bf16[1,128,4096]{2,1,0:T(8,128)(2,1)S(1)} %collective-permute-done.refs_1_.refs_3_, s32[1,256]{1,0:T(1,128)} %refs_4_.2, ...), custom_call_target="tpu_custom_call" | custom-call | flops 2952790016 | bytes 2621440 | tf_op jit(solution)/shard_map/pallas_call | solution.py:268
  49.6 0.0 copy-start.1
  49.6 0.0 collective-permute-start.1
  49.7 0.1 broadcast_in_dim.40
  49.8 0.9 %copy-done.1 = bf16[1,128,2048]{2,1,0:T(8,128)(2,1)S(1)} copy-done((bf16[1,128,2048]{2,1,0:T(8,128)(2,1)S(1)}, bf16[1,128,2048]{2,1,0:T(8,128)(2,1)}, u32[]{:S(2)}) %copy-start.1) | copy-done | bytes 524312
  50.7 1.1 %collective-permute-done.1 = bf16[1,128,2048]{2,1,0:T(8,128)(2,1)S(1)} collective-permute-done((bf16[1,128,2048]{2,1,0:T(8,128)(2,1)}, bf16[1,128,2048]{2,1,0:T(8,128)(2,1)S(1)}, u32[]{:S(2)}, u32[]{:S(2)}) %collective-permute-start.1) | collective-permute-done | bytes 524320 | tf_op jit(solution)/shard_map/ppermute | solution.py:296
  51.8 0.0 copy-start
  51.9 4.3 %all-to-all-done.1 = f16[16,136,128]{2,1,0:T(8,128)(2,1)S(1)} async-done(((f16[16,136,128]{2,1,0:T(8,128)(2,1)}), f16[16,136,128]{2,1,0:T(8,128)(2,1)S(1)}, u32[]{:S(2)}, u32[]{:S(2)}) %all-to-all-start.1) | async-done | bytes 557088 | tf_op jit(solution)/shard_map/all_to_all | solution.py:300
  56.1 0.1 convert_element_type.13.pieces_ref
  56.2 1.0 %shard_map.141 = (f32[2048,128]{1,0:T(8,128)}, f32[16,128]{1,0:T(8,128)}) custom-call(f32[16,136,128]{2,1,0:T(8,128)S(1)} %convert_element_type.13.pieces_ref), custom_call_target="tpu_custom_call" | custom-call | tf_op jit(solution)/shard_map/pallas_call | solution.py:325
  57.2 0.0 copy-done
  (7 shorter events, 0.2 us)
Async XLA Ops:
  0.6 3.8 %collective-permute-start = (bf16[1,128,4096]{2,1,0:T(8,128)(2,1)}, bf16[1,128,4096]{2,1,0:T(8,128)(2,1)S(1)}, u32[]{:S(2)}, u32[]{:S(2)}) collective-permute-start(bf16[1,128,4096]{2,1,0:T(8,128)(2,1)} %refs_2_.3), channel_id=1, source_target_pairs={{0,1},{1,0},{2,3},{3,2},{4,5},{5,4},{6,7},{7,6},{8,9},{9,8},{10,11... | collective-permute-start | bytes 3145736 | tf_op jit(solution)/shard_map/ppermute | solution.py:296
  2.3 2.2 %collective-permute-start.2 = (bf16[1,128,2048]{2,1,0:T(8,128)(2,1)S(1)}, bf16[1,128,2048]{2,1,0:T(8,128)(2,1)S(1)}, u32[]{:S(2)}, u32[]{:S(2)}) collective-permute-start(bf16[1,128,2048]{2,1,0:T(8,128)(2,1)S(1)} %constant_dynamic-slice_fusion), channel_id=1, source_target_pairs={{0,1},{1,0},{2,3},{3,2},{4,5},{5,4},{6,7},{7,6},{8,9},{9,8},{10,11... | collective-permute-start | bytes 1572872 | tf_op jit(solution)/shard_map/ppermute | solution.py:296
  11.3 24.2 %all-to-all-start = ((f16[16,136,128]{2,1,0:T(8,128)(2,1)}), f16[16,136,128]{2,1,0:T(8,128)(2,1)S(1)}, u32[]{:S(2)}, u32[]{:S(2)}) async-start(f16[16,136,128]{2,1,0:T(8,128)(2,1)} %convert_element_type.11), calls=%async_computation | async-start | bytes 1114112 | tf_op jit(solution)/shard_map/all_to_all | solution.py:300
  37.1 19.0 %all-to-all-start.1 = ((f16[16,136,128]{2,1,0:T(8,128)(2,1)}), f16[16,136,128]{2,1,0:T(8,128)(2,1)S(1)}, u32[]{:S(2)}, u32[]{:S(2)}) async-start(f16[16,136,128]{2,1,0:T(8,128)(2,1)} %broadcast_in_dim.46), calls=%async_computation.1 | async-start | bytes 1114112 | tf_op jit(solution)/shard_map/all_to_all | solution.py:300
  49.6 1.0 %copy-start.1 = (bf16[1,128,2048]{2,1,0:T(8,128)(2,1)S(1)}, bf16[1,128,2048]{2,1,0:T(8,128)(2,1)}, u32[]{:S(2)}) copy-start(bf16[1,128,2048]{2,1,0:T(8,128)(2,1)} %get-tuple-element.7) | copy-start | bytes 1572868
  49.6 2.2 %collective-permute-start.1 = (bf16[1,128,2048]{2,1,0:T(8,128)(2,1)}, bf16[1,128,2048]{2,1,0:T(8,128)(2,1)S(1)}, u32[]{:S(2)}, u32[]{:S(2)}) collective-permute-start(bf16[1,128,2048]{2,1,0:T(8,128)(2,1)} %get-tuple-element.8), channel_id=1, source_target_pairs={{0,1},{1,0},{2,3},{3,2},{4,5},{5,4},{6,7},{7,6},{8,9},{9,8},{10,11... | collective-permute-start | bytes 1572872 | tf_op jit(solution)/shard_map/ppermute | solution.py:296
  51.8 5.4 %copy-start = (bf16[1,128,4096]{2,1,0:T(8,128)(2,1)}, bf16[1,128,4096]{2,1,0:T(8,128)(2,1)S(1)}, u32[]{:S(2)}) copy-start(bf16[1,128,4096]{2,1,0:T(8,128)(2,1)S(1)} %constant_dynamic-update-slice_fusion) | copy-start | bytes 3145732
